TPU v7x, 32 devices: a whole 2x2x4 slice. The times are simulated.
32 devices in a mesh: sect: 4 (over z), dom: 8 (over y, x, core).
Axes of the slice: x: 2, y: 2, z: 4, core: 2. Of those that a mesh axis runs over, the one named last changes fastest.
Arguments:
- state: float32 [2048, 4096], P('sect', 'dom'), may hold values from -6 to 6
- previous: float32 [2048, 4096], P('sect', 'dom'), may hold values from -6 to 6
- coefficient: float32 [2048, 4096], P('sect', 'dom'), may hold values from 0.1 to 0.4
- stiffness: bfloat16 [4, 128, 128], replicated, may hold values from -1 to 1, as said below
- waveform: float32 [8, 32, 512], P(None, ('sect', 'dom')), may hold values from -6 to 6
- entry_face: int32 [1024], P(('sect', 'dom')), may hold values from 0 to 3
- entry_owner: int32 [1024, 1], P(('sect', 'dom')), may hold values from 0 to 7; in each aligned block of 32 rows (0 to 31, 32 to 63, ...) at most 8 rows name the same one
- entry_node: int32 [1024], P(('sect', 'dom')), may hold values from 0 to 3
- rbf: float32 [1024, 128, 128], P(('sect', 'dom')), may hold values from -0.109375 to 0.109375
Outputs:
- state_next: float32 [2048, 4096], P('sect', 'dom')
- previous_next: float32 [2048, 4096], P('sect', 'dom')
- waveform_next: float32 [8, 32, 512], P(None, ('sect', 'dom'))
Inputs may be any that keep to these rules, and one draw needn't show every extreme that they name: `entry_owner`: among the entries of one device, at most 8 name the same owner. `stiffness`: each element block is symmetric.
All inputs are finite; a program needn't handle non-finite values.
Results may differ from a plain program's by a relative error of at most 0.0006.
Values sent between devices are 32-bit elements; how exact they have to be, the bound alone decides.
A program may use at most 64 MiB of HBM per device.

v0:
```python
import jax
import jax.numpy as jnp
from jax import lax
from jax.sharding import PartitionSpec as P


def padded_2(block, sides, width):
    for axis, dim in sides:
        count = lax.axis_size(axis)
        forward = [(i, i + 1) for i in range(count - 1)]
        backward = [(target, source) for source, target in forward]
        low = lax.ppermute(
            lax.slice_in_dim(block, block.shape[dim] - width, None, axis=dim), axis, forward
        )
        high = lax.ppermute(lax.slice_in_dim(block, 0, width, axis=dim), axis, backward)
        block = jnp.concatenate([low, block, high], axis=dim)
    return block


def spread(value, axis, source):
    kept = jnp.where(lax.axis_index(axis) == source, value, 0).astype(value.dtype)
    return lax.psum(kept, axis)


def element_rows(field, stiffness):
    elem_blocks = stiffness.shape[0]
    elem_size = stiffness.shape[1]
    width = field.shape[1]
    rounded = field.astype(jnp.bfloat16).reshape(elem_blocks, elem_size, width)
    product = jnp.einsum("bic,bij->bjc", rounded, stiffness, preferred_element_type=jnp.float32)
    return product.reshape(elem_blocks * elem_size, width)


def local(
    state, previous, coefficient, stiffness, waveform, entry_face, entry_owner, entry_node, rbf
):
    row_count, lane_count = state.shape
    substeps = waveform.shape[0]
    n_sect = lax.axis_size("sect")
    n_dom = lax.axis_size("dom")
    section = lax.axis_index("sect")
    on_shell = section == n_sect - 1
    entries = rbf.shape[0]
    block_size = rbf.shape[1]
    block_count = lane_count // block_size
    capacity = max(2, 2 * entries // n_dom)
    highest = lax.Precision.HIGHEST
    iface_row = jnp.where(on_shell, 0, row_count - 1)
    row_ids = lax.broadcasted_iota(jnp.int32, (row_count, 1), 0)
    on_row = (row_ids == iface_row).astype(jnp.float32)
    keep_upper = jnp.where(section == n_sect - 1, 0.0, 1.0)
    keep_lower = jnp.where(section == n_sect - 2, 0.0, 1.0)
    current, before = (state, previous)
    traces = []
    for substep in range(substeps):
        padded = padded_2(current, (("sect", 0), ("dom", 1)), 1)
        upward = jnp.concatenate([padded[:1, 1:-1] * keep_upper, padded[1:-2, 1:-1]], 0)
        downward = jnp.concatenate([padded[2:-1, 1:-1], padded[-1:, 1:-1] * keep_lower], 0)
        near = upward + downward
        near = near + padded[1:-1, :-2] + padded[1:-1, 2:]
        laplace = near - 4.0 * current
        source = on_row * waveform[substep]
        element_term = lax.cond(
            on_shell,
            lambda: element_rows(current, stiffness),
            lambda: jnp.zeros((row_count, lane_count), jnp.float32),
        )
        updated = 2.0 * current - before + coefficient * (laplace - element_term + source)
        before, current = (current, updated)
        traces.append(lax.dynamic_slice_in_dim(current, iface_row, 1, 0)[0])
    trace_all = jnp.stack(traces)
    fluid_keep = jnp.where(on_shell, 0.0, 1.0)
    fluid_keep_int = jnp.where(on_shell, 0, 1)
    face_hot = (entry_face[:, None] == jnp.arange(block_count, dtype=jnp.int32)[None, :]).astype(
        jnp.float32
    )
    owner_index = entry_owner[:, 0]
    owner_hot = (owner_index[:, None] == jnp.arange(n_dom, dtype=jnp.int32)[None, :]).astype(
        jnp.int32
    )
    earlier = jnp.cumsum(owner_hot, 0) - owner_hot
    rank_index = jnp.sum(earlier * owner_hot, 1)
    slot_index = owner_index * capacity + rank_index
    slot_hot_int = (
        slot_index[:, None] == jnp.arange(n_dom * capacity, dtype=jnp.int32)[None, :]
    ).astype(jnp.int32)
    slot_hot = slot_hot_int.astype(jnp.float32)
    picked = jnp.einsum(
        "eb,kbf->ekf",
        face_hot,
        trace_all.reshape(substeps, block_count, block_size),
        precision=highest,
    )
    contribution = jnp.einsum("ekf,efn->ekn", picked, rbf, precision=highest)
    outgoing = jnp.einsum("es,ekn->skn", slot_hot, contribution, precision=highest) * fluid_keep
    slot_ids = jnp.sum(slot_hot_int * (entry_node + 1)[:, None], 0) * fluid_keep_int
    arrived, arrived_ids = (
        lax.all_to_all(
            outgoing.reshape(n_dom, capacity, substeps, block_size),
            "dom",
            split_axis=0,
            concat_axis=0,
            tiled=True,
        ),
        lax.all_to_all(
            slot_ids.reshape(n_dom, capacity), "dom", split_axis=0, concat_axis=0, tiled=True
        ),
    )
    arrived = arrived.reshape(n_dom * capacity, substeps, block_size)
    arrived_ids = arrived_ids.reshape(n_dom * capacity)
    node_hot = (
        (arrived_ids - 1)[:, None] == jnp.arange(block_count, dtype=jnp.int32)[None, :]
    ).astype(jnp.float32)
    partial_loads = jnp.einsum("sb,skn->kbn", node_hot, arrived, precision=highest).reshape(
        substeps, lane_count
    )
    node_loads = lax.psum(partial_loads, "sect")
    shell_trace = spread(trace_all, "sect", n_sect - 1)
    replies = jnp.einsum(
        "sb,kbn->skn",
        node_hot,
        shell_trace.reshape(substeps, block_count, block_size),
        precision=highest,
    )
    from_shell = lax.all_to_all(
        replies.reshape(n_dom, capacity, substeps, block_size),
        "dom",
        split_axis=0,
        concat_axis=0,
        tiled=True,
    )
    from_shell = from_shell.reshape(n_dom * capacity, substeps, block_size)
    fetched = jnp.einsum("es,skn->ekn", slot_hot, from_shell, precision=highest)
    face_terms = jnp.einsum("ekn,efn->ekf", fetched, rbf, precision=highest)
    face_disp = jnp.einsum("eb,ekf->kbf", face_hot, face_terms, precision=highest).reshape(
        substeps, lane_count
    )
    waveform_next = jnp.where(on_shell, node_loads, face_disp)[:, None, :]
    return (current, before, waveform_next)


def solution(mesh):
    in_specs = (
        P("sect", "dom"),
        P("sect", "dom"),
        P("sect", "dom"),
        P(),
        P(None, ("sect", "dom"), None),
        P(("sect", "dom")),
        P(("sect", "dom"), None),
        P(("sect", "dom")),
        P(("sect", "dom"), None, None),
    )
    out_specs = (P("sect", "dom"), P("sect", "dom"), P(None, ("sect", "dom"), None))
    return jax.shard_map(local, mesh=mesh, in_specs=in_specs, out_specs=out_specs, check_vma=False)
```

profile of v0, /device:TPU:0, one launch (start us, length us, event | category | flops | bytes accessed | tf_op | source)
XLA Modules:
  0.0 252.3 jit_solution(7093126265340989218)
XLA Ops:
  2.8 5.6 %collective-permute-start = (f32[1,512]{1,0:T(1,128)S(1)}, f32[1,512]{1,0:T(1,128)S(1)}, u32[]{:S(2)}, u32[]{:S(2)}) collective-permute-start(f32[1,512]{1,0:T(1,128)S(1)} %get-tuple-element.178), channel_id=1, source_target_pairs={{0,8},{8,16},{16,24},{1,9},{9,17},{17,25},{2,10},{10,18},{18,26},{... | collective-permute-start | bytes 6152 | tf_op jit(solution)/shard_map/ppermute | solution.py:12
  12.1 4.2 %all-to-all-start.1 = ((s32[8,1,8]{2,1,0:T(1,128)}), s32[8,1,8]{2,1,0:T(1,128)S(1)}, u32[]{:S(2)}, u32[]{:S(2)}) async-start(s32[8,1,8]{2,1,0:T(1,128)} %bitcast.31), calls=%async_computation.1 | async-start | bytes 8192 | tf_op jit(solution)/shard_map/all_to_all | solution.py:105
  32.1 4.5 %collective-permute-start.4 = (f32[1,512]{1,0:T(1,128)S(1)}, f32[1,512]{1,0:T(1,128)S(1)}, u32[]{:S(2)}, u32[]{:S(2)}) collective-permute-start(f32[1,512]{1,0:T(1,128)S(1)} %get-tuple-element.161), channel_id=1, source_target_pairs={{0,8},{8,16},{16,24},{1,9},{9,17},{17,25},{2,10},{10,18},{18,26},{... | collective-permute-start | bytes 6152 | tf_op jit(solution)/shard_map/ppermute | solution.py:12
  41.8 5.9 %collective-permute-start.6 = (f32[514,1]{1,0:T(8,128)S(1)}, f32[514,1]{1,0:T(8,128)S(1)}, u32[]{:S(2)}, u32[]{:S(2)}) collective-permute-start(f32[514,1]{1,0:T(8,128)S(1)} %get-tuple-element.137), channel_id=1, source_target_pairs={{0,1},{1,2},{2,3},{3,4},{4,5},{5,6},{6,7},{8,9},{9,10},{10,11},{11... | collective-permute-start | bytes 6176 | tf_op jit(solution)/shard_map/ppermute | solution.py:12
  53.6 4.5 %collective-permute-start.8 = (f32[1,512]{1,0:T(1,128)S(1)}, f32[1,512]{1,0:T(1,128)S(1)}, u32[]{:S(2)}, u32[]{:S(2)}) collective-permute-start(f32[1,512]{1,0:T(1,128)S(1)} %get-tuple-element.158), channel_id=1, source_target_pairs={{0,8},{8,16},{16,24},{1,9},{9,17},{17,25},{2,10},{10,18},{18,26},{... | collective-permute-start | bytes 6152 | tf_op jit(solution)/shard_map/ppermute | solution.py:12
  63.3 7.2 %collective-permute-start.10 = (f32[514,1]{1,0:T(8,128)S(1)}, f32[514,1]{1,0:T(8,128)S(1)}, u32[]{:S(2)}, u32[]{:S(2)}) collective-permute-start(f32[514,1]{1,0:T(8,128)S(1)} %get-tuple-element.135), channel_id=1, source_target_pairs={{0,1},{1,2},{2,3},{3,4},{4,5},{5,6},{6,7},{8,9},{9,10},{10,11},{11... | collective-permute-start | bytes 6176 | tf_op jit(solution)/shard_map/ppermute | solution.py:12
  76.4 4.5 %collective-permute-start.12 = (f32[1,512]{1,0:T(1,128)S(1)}, f32[1,512]{1,0:T(1,128)S(1)}, u32[]{:S(2)}, u32[]{:S(2)}) collective-permute-start(f32[1,512]{1,0:T(1,128)S(1)} %get-tuple-element.155), channel_id=1, source_target_pairs={{0,8},{8,16},{16,24},{1,9},{9,17},{17,25},{2,10},{10,18},{18,26},{... | collective-permute-start | bytes 6152 | tf_op jit(solution)/shard_map/ppermute | solution.py:12
  86.1 7.2 %collective-permute-start.14 = (f32[514,1]{1,0:T(8,128)S(1)}, f32[514,1]{1,0:T(8,128)S(1)}, u32[]{:S(2)}, u32[]{:S(2)}) collective-permute-start(f32[514,1]{1,0:T(8,128)S(1)} %get-tuple-element.133), channel_id=1, source_target_pairs={{0,1},{1,2},{2,3},{3,4},{4,5},{5,6},{6,7},{8,9},{9,10},{10,11},{11... | collective-permute-start | bytes 6176 | tf_op jit(solution)/shard_map/ppermute | solution.py:12
  99.2 4.5 %collective-permute-start.16 = (f32[1,512]{1,0:T(1,128)S(1)}, f32[1,512]{1,0:T(1,128)S(1)}, u32[]{:S(2)}, u32[]{:S(2)}) collective-permute-start(f32[1,512]{1,0:T(1,128)S(1)} %get-tuple-element.152), channel_id=1, source_target_pairs={{0,8},{8,16},{16,24},{1,9},{9,17},{17,25},{2,10},{10,18},{18,26},{... | collective-permute-start | bytes 6152 | tf_op jit(solution)/shard_map/ppermute | solution.py:12
  109.0 7.2 %collective-permute-start.18 = (f32[514,1]{1,0:T(8,128)S(1)}, f32[514,1]{1,0:T(8,128)S(1)}, u32[]{:S(2)}, u32[]{:S(2)}) collective-permute-start(f32[514,1]{1,0:T(8,128)S(1)} %get-tuple-element.131), channel_id=1, source_target_pairs={{0,1},{1,2},{2,3},{3,4},{4,5},{5,6},{6,7},{8,9},{9,10},{10,11},{11... | collective-permute-start | bytes 6176 | tf_op jit(solution)/shard_map/ppermute | solution.py:12
  117.3 3.9 %fusion.27 = f32[512,512]{1,0:T(8,128)S(1)} fusion(f32[512,512]{1,0:T(8,128)S(1)} %copy-done.1, f32[512,512]{1,0:T(8,128)} %get-tuple-element.194, f32[514,1]{1,0:T(8,128)S(1)} %collective-permute-done.19, f32[1,512]{1,0:T(1,128)S(1)} %collective-permute-done.17, f32[512,512]{1,0:T(8,128)} %copy-done.8, f32[1,512]{1,0:T(1,128)S(1)} %collective-permute-done.16, ...), kind=kLoop, calls=%fused_computation.49 | loop fusion | flops 5242880 | bytes 7352336 | tf_op jit(solution)/shard_map/add | solution.py:68
  122.6 4.5 %collective-permute-start.20 = (f32[1,512]{1,0:T(1,128)S(1)}, f32[1,512]{1,0:T(1,128)S(1)}, u32[]{:S(2)}, u32[]{:S(2)}) collective-permute-start(f32[1,512]{1,0:T(1,128)S(1)} %get-tuple-element.149), channel_id=1, source_target_pairs={{0,8},{8,16},{16,24},{1,9},{9,17},{17,25},{2,10},{10,18},{18,26},{... | collective-permute-start | bytes 6152 | tf_op jit(solution)/shard_map/ppermute | solution.py:12
  132.3 7.2 %collective-permute-start.22 = (f32[514,1]{1,0:T(8,128)S(1)}, f32[514,1]{1,0:T(8,128)S(1)}, u32[]{:S(2)}, u32[]{:S(2)}) collective-permute-start(f32[514,1]{1,0:T(8,128)S(1)} %get-tuple-element.129), channel_id=1, source_target_pairs={{0,1},{1,2},{2,3},{3,4},{4,5},{5,6},{6,7},{8,9},{9,10},{10,11},{11... | collective-permute-start | bytes 6176 | tf_op jit(solution)/shard_map/ppermute | solution.py:12
  140.7 3.9 %fusion.20 = f32[512,512]{1,0:T(8,128)S(1)} fusion(f32[512,512]{1,0:T(8,128)S(1)} %copy-done.1, f32[512,512]{1,0:T(8,128)} %get-tuple-element.195, f32[514,1]{1,0:T(8,128)S(1)} %collective-permute-done.23, f32[1,512]{1,0:T(1,128)S(1)} %collective-permute-done.21, f32[512,512]{1,0:T(8,128)} %copy-done.10, f32[1,512]{1,0:T(1,128)S(1)} %collective-permute-done.20, ...), kind=kLoop, calls=%fused_computation.36 | loop fusion | flops 5242880 | bytes 7352336 | tf_op jit(solution)/shard_map/add | solution.py:68
  145.9 4.5 %collective-permute-start.24 = (f32[1,512]{1,0:T(1,128)S(1)}, f32[1,512]{1,0:T(1,128)S(1)}, u32[]{:S(2)}, u32[]{:S(2)}) collective-permute-start(f32[1,512]{1,0:T(1,128)S(1)} %get-tuple-element.146), channel_id=1, source_target_pairs={{0,8},{8,16},{16,24},{1,9},{9,17},{17,25},{2,10},{10,18},{18,26},{... | collective-permute-start | bytes 6152 | tf_op jit(solution)/shard_map/ppermute | solution.py:12
  155.7 7.2 %collective-permute-start.26 = (f32[514,1]{1,0:T(8,128)S(1)}, f32[514,1]{1,0:T(8,128)S(1)}, u32[]{:S(2)}, u32[]{:S(2)}) collective-permute-start(f32[514,1]{1,0:T(8,128)S(1)} %get-tuple-element.127), channel_id=1, source_target_pairs={{0,1},{1,2},{2,3},{3,4},{4,5},{5,6},{6,7},{8,9},{9,10},{10,11},{11... | collective-permute-start | bytes 6176 | tf_op jit(solution)/shard_map/ppermute | solution.py:12
  164.0 3.4 %fusion.13 = f32[512,512]{1,0:T(8,128)S(1)} fusion(f32[512,512]{1,0:T(8,128)S(1)} %copy-done.1, f32[512,512]{1,0:T(8,128)} %get-tuple-element.196, f32[514,1]{1,0:T(8,128)S(1)} %collective-permute-done.27, f32[1,512]{1,0:T(1,128)S(1)} %collective-permute-done.25, f32[512,512]{1,0:T(8,128)S(1)} %copy-done.3, f32[1,512]{1,0:T(1,128)S(1)} %collective-permute-done.24, ...), kind=kLoop, calls=%fused_computation.23 | loop fusion | flops 5242880 | bytes 7352336 | tf_op jit(solution)/shard_map/add | solution.py:68
  168.7 4.5 %collective-permute-start.28 = (f32[1,512]{1,0:T(1,128)S(1)}, f32[1,512]{1,0:T(1,128)S(1)}, u32[]{:S(2)}, u32[]{:S(2)}) collective-permute-start(f32[1,512]{1,0:T(1,128)S(1)} %get-tuple-element.143), channel_id=1, source_target_pairs={{0,8},{8,16},{16,24},{1,9},{9,17},{17,25},{2,10},{10,18},{18,26},{... | collective-permute-start | bytes 6152 | tf_op jit(solution)/shard_map/ppermute | solution.py:12
  178.5 7.2 %collective-permute-start.30 = (f32[514,1]{1,0:T(8,128)S(1)}, f32[514,1]{1,0:T(8,128)S(1)}, u32[]{:S(2)}, u32[]{:S(2)}) collective-permute-start(f32[514,1]{1,0:T(8,128)S(1)} %get-tuple-element.125), channel_id=1, source_target_pairs={{0,1},{1,2},{2,3},{3,4},{4,5},{5,6},{6,7},{8,9},{9,10},{10,11},{11... | collective-permute-start | bytes 6176 | tf_op jit(solution)/shard_map/ppermute | solution.py:12
  186.9 3.9 %fusion.6 = f32[512,512]{1,0:T(8,128)S(1)} fusion(f32[512,512]{1,0:T(8,128)S(1)} %copy-done.1, f32[512,512]{1,0:T(8,128)} %get-tuple-element.197, f32[514,1]{1,0:T(8,128)S(1)} %collective-permute-done.31, f32[1,512]{1,0:T(1,128)S(1)} %collective-permute-done.29, f32[512,512]{1,0:T(8,128)} %copy-done.15, f32[1,512]{1,0:T(1,128)S(1)} %collective-permute-done.28, ...), kind=kLoop, calls=%fused_computation.10 | loop fusion | flops 5242880 | bytes 7352336 | tf_op jit(solution)/shard_map/add | solution.py:68
  195.1 17.2 %all-to-all-start = ((f32[8,8,8,128]{3,1,2,0:T(8,128)}), f32[8,8,8,128]{3,1,2,0:T(8,128)S(1)}, u32[]{:S(2)}, u32[]{:S(2)}) async-start(f32[8,8,8,128]{3,1,2,0:T(8,128)} %copy.39), calls=%async_computation | async-start | bytes 524288 | tf_op jit(solution)/shard_map/all_to_all | solution.py:98
  212.5 6.8 %all-to-all-done = f32[8,8,8,128]{3,1,2,0:T(8,128)S(1)} async-done(((f32[8,8,8,128]{3,1,2,0:T(8,128)}), f32[8,8,8,128]{3,1,2,0:T(8,128)S(1)}, u32[]{:S(2)}, u32[]{:S(2)}) %all-to-all-start) | async-done | bytes 262176 | tf_op jit(solution)/shard_map/all_to_all | solution.py:98
  219.5 18.6 %all-reduce = (f32[8,512]{1,0:T(8,128)S(1)}, f32[8,4,128]{2,1,0:T(4,128)S(1)}) all-reduce(f32[8,512]{1,0:T(8,128)S(1)} %bitcast.111, f32[8,4,128]{2,1,0:T(4,128)S(1)} %reshape.149), channel_id=1, replica_groups=mesh['sect'=4,'dom'=8] {'sect'}, use_global_device_ids=true, to_apply=%region_19.20 | all-reduce | flops 8192 | bytes 65536 | tf_op jit(solution)/shard_map/psum | solution.py:117
  238.4 9.3 %all_to_all.16 = f32[8,8,8,128]{3,1,2,0:T(8,128)S(1)} all-to-all(f32[8,8,8,128]{3,1,2,0:T(8,128)S(1)} %fusion.67), channel_id=1, replica_groups=mesh['sect'=4,'dom'=8] {'dom'}, dimensions={0} | all-to-all | bytes 524288 | tf_op jit(solution)/shard_map/all_to_all | solution.py:125
  (182 shorter events, 101.8 us)
Async XLA Ops:
  1.5 19.1 %collective-permute-start.1 = (f32[1,512]{1,0:T(1,128)S(1)}, f32[1,512]{1,0:T(1,128)S(1)}, u32[]{:S(2)}, u32[]{:S(2)}) collective-permute-start(f32[1,512]{1,0:T(1,128)S(1)} %get-tuple-element.179), channel_id=1, source_target_pairs={{8,0},{16,8},{24,16},{9,1},{17,9},{25,17},{10,2},{18,10},{26,18},{... | collective-permute-start | bytes 6152 | tf_op jit(solution)/shard_map/ppermute | solution.py:15
  2.8 17.8 %collective-permute-start = (f32[1,512]{1,0:T(1,128)S(1)}, f32[1,512]{1,0:T(1,128)S(1)}, u32[]{:S(2)}, u32[]{:S(2)}) collective-permute-start(f32[1,512]{1,0:T(1,128)S(1)} %get-tuple-element.178), channel_id=1, source_target_pairs={{0,8},{8,16},{16,24},{1,9},{9,17},{17,25},{2,10},{10,18},{18,26},{... | collective-permute-start | bytes 6152 | tf_op jit(solution)/shard_map/ppermute | solution.py:12
  12.1 183.0 %all-to-all-start.1 = ((s32[8,1,8]{2,1,0:T(1,128)}), s32[8,1,8]{2,1,0:T(1,128)S(1)}, u32[]{:S(2)}, u32[]{:S(2)}) async-start(s32[8,1,8]{2,1,0:T(1,128)} %bitcast.31), calls=%async_computation.1 | async-start | bytes 8192 | tf_op jit(solution)/shard_map/all_to_all | solution.py:105
  30.8 8.5 %collective-permute-start.5 = (f32[1,512]{1,0:T(1,128)S(1)}, f32[1,512]{1,0:T(1,128)S(1)}, u32[]{:S(2)}, u32[]{:S(2)}) collective-permute-start(f32[1,512]{1,0:T(1,128)S(1)} %get-tuple-element.160), channel_id=1, source_target_pairs={{8,0},{16,8},{24,16},{9,1},{17,9},{25,17},{10,2},{18,10},{26,18},{... | collective-permute-start | bytes 6152 | tf_op jit(solution)/shard_map/ppermute | solution.py:15
  40.5 7.2 %collective-permute-start.7 = (f32[514,1]{1,0:T(8,128)S(1)}, f32[514,1]{1,0:T(8,128)S(1)}, u32[]{:S(2)}, u32[]{:S(2)}) collective-permute-start(f32[514,1]{1,0:T(8,128)S(1)} %get-tuple-element.138), channel_id=1, source_target_pairs={{1,0},{2,1},{3,2},{4,3},{5,4},{6,5},{7,6},{9,8},{10,9},{11,10},{12... | collective-permute-start | bytes 6176 | tf_op jit(solution)/shard_map/ppermute | solution.py:15
  52.3 8.5 %collective-permute-start.9 = (f32[1,512]{1,0:T(1,128)S(1)}, f32[1,512]{1,0:T(1,128)S(1)}, u32[]{:S(2)}, u32[]{:S(2)}) collective-permute-start(f32[1,512]{1,0:T(1,128)S(1)} %get-tuple-element.157), channel_id=1, source_target_pairs={{8,0},{16,8},{24,16},{9,1},{17,9},{25,17},{10,2},{18,10},{26,18},{... | collective-permute-start | bytes 6152 | tf_op jit(solution)/shard_map/ppermute | solution.py:15
  62.0 8.6 %collective-permute-start.11 = (f32[514,1]{1,0:T(8,128)S(1)}, f32[514,1]{1,0:T(8,128)S(1)}, u32[]{:S(2)}, u32[]{:S(2)}) collective-permute-start(f32[514,1]{1,0:T(8,128)S(1)} %get-tuple-element.136), channel_id=1, source_target_pairs={{1,0},{2,1},{3,2},{4,3},{5,4},{6,5},{7,6},{9,8},{10,9},{11,10},{12... | collective-permute-start | bytes 6176 | tf_op jit(solution)/shard_map/ppermute | solution.py:15
  63.3 8.4 %collective-permute-start.10 = (f32[514,1]{1,0:T(8,128)S(1)}, f32[514,1]{1,0:T(8,128)S(1)}, u32[]{:S(2)}, u32[]{:S(2)}) collective-permute-start(f32[514,1]{1,0:T(8,128)S(1)} %get-tuple-element.135), channel_id=1, source_target_pairs={{0,1},{1,2},{2,3},{3,4},{4,5},{5,6},{6,7},{8,9},{9,10},{10,11},{11... | collective-permute-start | bytes 6176 | tf_op jit(solution)/shard_map/ppermute | solution.py:12
  75.1 8.5 %collective-permute-start.13 = (f32[1,512]{1,0:T(1,128)S(1)}, f32[1,512]{1,0:T(1,128)S(1)}, u32[]{:S(2)}, u32[]{:S(2)}) collective-permute-start(f32[1,512]{1,0:T(1,128)S(1)} %get-tuple-element.154), channel_id=1, source_target_pairs={{8,0},{16,8},{24,16},{9,1},{17,9},{25,17},{10,2},{18,10},{26,18},{... | collective-permute-start | bytes 6152 | tf_op jit(solution)/shard_map/ppermute | solution.py:15
  84.8 8.6 %collective-permute-start.15 = (f32[514,1]{1,0:T(8,128)S(1)}, f32[514,1]{1,0:T(8,128)S(1)}, u32[]{:S(2)}, u32[]{:S(2)}) collective-permute-start(f32[514,1]{1,0:T(8,128)S(1)} %get-tuple-element.134), channel_id=1, source_target_pairs={{1,0},{2,1},{3,2},{4,3},{5,4},{6,5},{7,6},{9,8},{10,9},{11,10},{12... | collective-permute-start | bytes 6176 | tf_op jit(solution)/shard_map/ppermute | solution.py:15
  86.1 8.4 %collective-permute-start.14 = (f32[514,1]{1,0:T(8,128)S(1)}, f32[514,1]{1,0:T(8,128)S(1)}, u32[]{:S(2)}, u32[]{:S(2)}) collective-permute-start(f32[514,1]{1,0:T(8,128)S(1)} %get-tuple-element.133), channel_id=1, source_target_pairs={{0,1},{1,2},{2,3},{3,4},{4,5},{5,6},{6,7},{8,9},{9,10},{10,11},{11... | collective-permute-start | bytes 6176 | tf_op jit(solution)/shard_map/ppermute | solution.py:12
  97.9 8.5 %collective-permute-start.17 = (f32[1,512]{1,0:T(1,128)S(1)}, f32[1,512]{1,0:T(1,128)S(1)}, u32[]{:S(2)}, u32[]{:S(2)}) collective-permute-start(f32[1,512]{1,0:T(1,128)S(1)} %get-tuple-element.151), channel_id=1, source_target_pairs={{8,0},{16,8},{24,16},{9,1},{17,9},{25,17},{10,2},{18,10},{26,18},{... | collective-permute-start | bytes 6152 | tf_op jit(solution)/shard_map/ppermute | solution.py:15
  107.7 8.6 %collective-permute-start.19 = (f32[514,1]{1,0:T(8,128)S(1)}, f32[514,1]{1,0:T(8,128)S(1)}, u32[]{:S(2)}, u32[]{:S(2)}) collective-permute-start(f32[514,1]{1,0:T(8,128)S(1)} %get-tuple-element.132), channel_id=1, source_target_pairs={{1,0},{2,1},{3,2},{4,3},{5,4},{6,5},{7,6},{9,8},{10,9},{11,10},{12... | collective-permute-start | bytes 6176 | tf_op jit(solution)/shard_map/ppermute | solution.py:15
  109.0 8.4 %collective-permute-start.18 = (f32[514,1]{1,0:T(8,128)S(1)}, f32[514,1]{1,0:T(8,128)S(1)}, u32[]{:S(2)}, u32[]{:S(2)}) collective-permute-start(f32[514,1]{1,0:T(8,128)S(1)} %get-tuple-element.131), channel_id=1, source_target_pairs={{0,1},{1,2},{2,3},{3,4},{4,5},{5,6},{6,7},{8,9},{9,10},{10,11},{11... | collective-permute-start | bytes 6176 | tf_op jit(solution)/shard_map/ppermute | solution.py:12
  121.3 8.5 %collective-permute-start.21 = (f32[1,512]{1,0:T(1,128)S(1)}, f32[1,512]{1,0:T(1,128)S(1)}, u32[]{:S(2)}, u32[]{:S(2)}) collective-permute-start(f32[1,512]{1,0:T(1,128)S(1)} %get-tuple-element.148), channel_id=1, source_target_pairs={{8,0},{16,8},{24,16},{9,1},{17,9},{25,17},{10,2},{18,10},{26,18},{... | collective-permute-start | bytes 6152 | tf_op jit(solution)/shard_map/ppermute | solution.py:15
  131.0 8.6 %collective-permute-start.23 = (f32[514,1]{1,0:T(8,128)S(1)}, f32[514,1]{1,0:T(8,128)S(1)}, u32[]{:S(2)}, u32[]{:S(2)}) collective-permute-start(f32[514,1]{1,0:T(8,128)S(1)} %get-tuple-element.130), channel_id=1, source_target_pairs={{1,0},{2,1},{3,2},{4,3},{5,4},{6,5},{7,6},{9,8},{10,9},{11,10},{12... | collective-permute-start | bytes 6176 | tf_op jit(solution)/shard_map/ppermute | solution.py:15
  132.3 8.4 %collective-permute-start.22 = (f32[514,1]{1,0:T(8,128)S(1)}, f32[514,1]{1,0:T(8,128)S(1)}, u32[]{:S(2)}, u32[]{:S(2)}) collective-permute-start(f32[514,1]{1,0:T(8,128)S(1)} %get-tuple-element.129), channel_id=1, source_target_pairs={{0,1},{1,2},{2,3},{3,4},{4,5},{5,6},{6,7},{8,9},{9,10},{10,11},{11... | collective-permute-start | bytes 6176 | tf_op jit(solution)/shard_map/ppermute | solution.py:12
  144.6 8.5 %collective-permute-start.25 = (f32[1,512]{1,0:T(1,128)S(1)}, f32[1,512]{1,0:T(1,128)S(1)}, u32[]{:S(2)}, u32[]{:S(2)}) collective-permute-start(f32[1,512]{1,0:T(1,128)S(1)} %get-tuple-element.145), channel_id=1, source_target_pairs={{8,0},{16,8},{24,16},{9,1},{17,9},{25,17},{10,2},{18,10},{26,18},{... | collective-permute-start | bytes 6152 | tf_op jit(solution)/shard_map/ppermute | solution.py:15
  154.4 8.6 %collective-permute-start.27 = (f32[514,1]{1,0:T(8,128)S(1)}, f32[514,1]{1,0:T(8,128)S(1)}, u32[]{:S(2)}, u32[]{:S(2)}) collective-permute-start(f32[514,1]{1,0:T(8,128)S(1)} %get-tuple-element.128), channel_id=1, source_target_pairs={{1,0},{2,1},{3,2},{4,3},{5,4},{6,5},{7,6},{9,8},{10,9},{11,10},{12... | collective-permute-start | bytes 6176 | tf_op jit(solution)/shard_map/ppermute | solution.py:15
  155.7 8.4 %collective-permute-start.26 = (f32[514,1]{1,0:T(8,128)S(1)}, f32[514,1]{1,0:T(8,128)S(1)}, u32[]{:S(2)}, u32[]{:S(2)}) collective-permute-start(f32[514,1]{1,0:T(8,128)S(1)} %get-tuple-element.127), channel_id=1, source_target_pairs={{0,1},{1,2},{2,3},{3,4},{4,5},{5,6},{6,7},{8,9},{9,10},{10,11},{11... | collective-permute-start | bytes 6176 | tf_op jit(solution)/shard_map/ppermute | solution.py:12
  167.4 8.5 %collective-permute-start.29 = (f32[1,512]{1,0:T(1,128)S(1)}, f32[1,512]{1,0:T(1,128)S(1)}, u32[]{:S(2)}, u32[]{:S(2)}) collective-permute-start(f32[1,512]{1,0:T(1,128)S(1)} %get-tuple-element.142), channel_id=1, source_target_pairs={{8,0},{16,8},{24,16},{9,1},{17,9},{25,17},{10,2},{18,10},{26,18},{... | collective-permute-start | bytes 6152 | tf_op jit(solution)/shard_map/ppermute | solution.py:15
  177.2 8.6 %collective-permute-start.31 = (f32[514,1]{1,0:T(8,128)S(1)}, f32[514,1]{1,0:T(8,128)S(1)}, u32[]{:S(2)}, u32[]{:S(2)}) collective-permute-start(f32[514,1]{1,0:T(8,128)S(1)} %get-tuple-element.126), channel_id=1, source_target_pairs={{1,0},{2,1},{3,2},{4,3},{5,4},{6,5},{7,6},{9,8},{10,9},{11,10},{12... | collective-permute-start | bytes 6176 | tf_op jit(solution)/shard_map/ppermute | solution.py:15
  178.5 8.4 %collective-permute-start.30 = (f32[514,1]{1,0:T(8,128)S(1)}, f32[514,1]{1,0:T(8,128)S(1)}, u32[]{:S(2)}, u32[]{:S(2)}) collective-permute-start(f32[514,1]{1,0:T(8,128)S(1)} %get-tuple-element.125), channel_id=1, source_target_pairs={{0,1},{1,2},{2,3},{3,4},{4,5},{5,6},{6,7},{8,9},{9,10},{10,11},{11... | collective-permute-start | bytes 6176 | tf_op jit(solution)/shard_map/ppermute | solution.py:12
  195.1 24.1 %all-to-all-start = ((f32[8,8,8,128]{3,1,2,0:T(8,128)}), f32[8,8,8,128]{3,1,2,0:T(8,128)S(1)}, u32[]{:S(2)}, u32[]{:S(2)}) async-start(f32[8,8,8,128]{3,1,2,0:T(8,128)} %copy.39), calls=%async_computation | async-start | bytes 524288 | tf_op jit(solution)/shard_map/all_to_all | solution.py:98
  (31 other events, 411.1 us)
where the time goes:
time: 254 us; the launch traced here: 252 us
  starting transfers between devices  132 us (52%)
  other arithmetic  41.8 us (16%)
  blocking collectives  27.9 us (11%)
  local copies, waits for them, and re-layouts  26.7 us (11%)
  waiting for transfers between devices  15.7 us (6%)
  matrix products  7.01 us (3%)
    ppermute x16, starting transfers between devices, padded_2(): lax.ppermute(lax.slice_in_dim(block, block.shape[dim] - width, None, axis...  89.7 us
    add x8, other arithmetic, local(): 2.0 * current - before + coefficient * (laplace - element_term + source)  28.6 us
    ppermute x16, starting transfers between devices, padded_2(): lax.ppermute(lax.slice_in_dim(block, 0, width, axis=dim), axis, backward)  20.7 us
    psum x1, blocking collectives, local(): node_loads = lax.psum(partial_loads, 'sect')  18.6 us
    all_to_all x1, starting transfers between devices, local(): lax.all_to_all(outgoing.reshape(n_dom, capacity, substeps, block_size), '...  17.2 us
    slice x8, local copies, waits for them, and re-layouts, local(): padded[2:-1, 1:-1]  13.6 us
    slice x8, other arithmetic, padded_2(): lax.slice_in_dim(block, block.shape[dim] - width, None, axis=dim)  10.1 us
    all_to_all x1, blocking collectives, local(): lax.all_to_all(replies.reshape(n_dom, capacity, substeps, block_size), 'd...  9.35 us
  transfers between devices with their start and end apart: 34, of which 9 were waited for; matrix products, arithmetic and copies ran while one was open for 27% of the time, Pallas kernels for 0%

commit v1 on v0

v1 whole, which is shorter than its diff:
```python
import functools

import jax
import jax.numpy as jnp
from jax import lax
from jax.experimental import pallas as pl
from jax.experimental.pallas import tpu as pltpu
from jax.sharding import PartitionSpec as P

HALO = 8
TILE = 128
F32 = jnp.float32
BF16 = jnp.bfloat16


def signal(barrier, section, column):
    pl.semaphore_signal(
        barrier, inc=1, device_id=(section, column), device_id_type=pl.DeviceIdType.MESH
    )


def remote(source, target, send, recv, section, column):
    return pltpu.make_async_remote_copy(
        src_ref=source,
        dst_ref=target,
        send_sem=send,
        recv_sem=recv,
        device_id=(section, column),
        device_id_type=pl.DeviceIdType.MESH,
    )


def halo_kernel(
    n_sect, n_dom, *refs
):
    lefts, rights, tops, bottoms = refs[0:3], refs[3:6], refs[6:9], refs[9:12]
    wave_ref = refs[12]
    sides_ref, wave_out, above_ref, below_ref = refs[13:17]
    (to_left, to_right, from_left, from_right, to_up, to_down, from_up, from_down) = refs[17:25]
    send_sem, recv_sem = refs[25:27]
    s = lax.axis_index("sect")
    d = lax.axis_index("dom")
    rows = sides_ref.shape[1]
    lanes = tops[0].shape[1]
    has_left = d > 0
    has_right = d < n_dom - 1
    has_up = jnp.logical_and(s >= 1, s <= n_sect - 2)
    has_down = s <= n_sect - 3
    places = (
        (has_left, s, d - 1),
        (has_right, s, d + 1),
        (has_up, s - 1, d),
        (has_down, s + 1, d),
    )
    barrier = pltpu.get_barrier_semaphore()
    for has, section, column in places:

        @pl.when(has)
        def _(section=section, column=column):
            signal(barrier, section, column)

    lane = lax.broadcasted_iota(jnp.int32, (rows, TILE), 1)

    def pack(tiles, start):
        a = tiles[0][...]
        b = pltpu.roll(tiles[1][...], (HALO - start) % TILE, 1)
        c = pltpu.roll(tiles[2][...], (2 * HALO - start) % TILE, 1)
        if start:
            a = pltpu.roll(a, TILE - start, 1)
        packed = jnp.where(lane < HALO, a, jnp.where(lane < 2 * HALO, b, c))
        return packed.T[: 3 * HALO]

    to_left[: 3 * HALO] = pack(lefts, 0)
    to_left[3 * HALO :, :TILE] = wave_ref[:, :TILE]
    to_left[3 * HALO :, TILE:] = jnp.zeros((HALO, rows - TILE), F32)
    to_right[: 3 * HALO] = pack(rights, TILE - HALO)
    to_right[3 * HALO :, :TILE] = wave_ref[:, lanes - TILE :]
    to_right[3 * HALO :, TILE:] = jnp.zeros((HALO, rows - TILE), F32)

    peers = sum(jnp.where(has, 1, 0).astype(jnp.int32) for has, _, _ in places)
    pl.semaphore_wait(barrier, peers)

    go_left = remote(to_left, from_right, send_sem.at[0], recv_sem.at[0], s, d - 1)
    go_right = remote(to_right, from_left, send_sem.at[1], recv_sem.at[1], s, d + 1)

    @pl.when(has_left)
    def _():
        go_left.start()

    @pl.when(has_right)
    def _():
        go_right.start()

    @pl.when(has_right)
    def _():
        go_left.wait_recv()

    @pl.when(jnp.logical_not(has_right))
    def _():
        from_right[...] = jnp.zeros_like(from_right)

    @pl.when(has_left)
    def _():
        go_right.wait_recv()

    @pl.when(jnp.logical_not(has_left))
    def _():
        from_left[...] = jnp.zeros_like(from_left)

    fill = jnp.zeros((TILE - 3 * HALO, rows), F32)
    right = jnp.concatenate([from_right[: 3 * HALO], fill], 0).T
    left = jnp.concatenate([from_left[: 3 * HALO], fill], 0).T
    for a in range(3):
        r = pltpu.roll(right, (TILE - a * HALO) % TILE, 1) if a else right
        le = pltpu.roll(left, TILE - (a + 1) * HALO, 1)
        sides_ref[a] = jnp.where(lane < HALO, r, jnp.where(lane >= TILE - HALO, le, 0.0))
        part = pl.ds(a * HALO, HALO)
        to_up[part, :lanes] = tops[a][...]
        to_up[part, lanes:] = sides_ref[a, :HALO]
        to_down[part, :lanes] = bottoms[a][...]
        to_down[part, lanes:] = sides_ref[a, rows - HALO :]
    lane8 = lane[:HALO]
    wave_side = jnp.where(
        lane8 < HALO,
        from_right[3 * HALO :, :TILE],
        jnp.where(lane8 >= TILE - HALO, from_left[3 * HALO :, :TILE], 0.0),
    )
    wave_out[:, :lanes] = wave_ref[...]
    wave_out[:, lanes:] = wave_side
    to_down[3 * HALO :, :lanes] = wave_ref[...]
    to_down[3 * HALO :, lanes:] = wave_side

    go_up = remote(to_up, from_down, send_sem.at[2], recv_sem.at[2], s - 1, d)
    go_down = remote(to_down, from_up, send_sem.at[3], recv_sem.at[3], s + 1, d)

    @pl.when(has_up)
    def _():
        go_up.start()

    @pl.when(has_down)
    def _():
        go_down.start()

    @pl.when(has_down)
    def _():
        go_up.wait_recv()
        below_ref[...] = from_down[...]

    @pl.when(jnp.logical_not(has_down))
    def _():
        below_ref[...] = jnp.zeros_like(below_ref)

    @pl.when(has_up)
    def _():
        go_down.wait_recv()
        above_ref[...] = from_up[...]

    @pl.when(jnp.logical_not(has_up))
    def _():
        above_ref[...] = jnp.zeros_like(above_ref)

    for has, copy in (
        (has_left, go_left),
        (has_right, go_right),
        (has_up, go_up),
        (has_down, go_down),
    ):

        @pl.when(has)
        def _(copy=copy):
            copy.wait_send()


def exchange(state, previous, coefficient, wave, n_sect, n_dom):
    rows, lanes = state.shape
    fields = (state, previous, coefficient)
    last = lanes // TILE - 1
    wide = lanes + TILE

    def spec(shape, where):
        return pl.BlockSpec(shape, lambda i: where)

    return pl.pallas_call(
        functools.partial(halo_kernel, n_sect, n_dom),
        grid=(1,),
        out_shape=(
            jax.ShapeDtypeStruct((3, rows, TILE), F32),
            jax.ShapeDtypeStruct((HALO, wide), F32),
            jax.ShapeDtypeStruct((4 * HALO, wide), F32),
            jax.ShapeDtypeStruct((3 * HALO, wide), F32),
        ),
        in_specs=[spec((rows, TILE), (0, 0))] * 3
        + [spec((rows, TILE), (0, last))] * 3
        + [spec((HALO, lanes), (0, 0))] * 3
        + [spec((HALO, lanes), (rows // HALO - 1, 0))] * 3
        + [spec((HALO, lanes), (0, 0))],
        out_specs=(
            pl.BlockSpec((3, rows, TILE), lambda i: (0, 0, 0)),
            spec((HALO, wide), (0, 0)),
            spec((4 * HALO, wide), (0, 0)),
            spec((3 * HALO, wide), (0, 0)),
        ),
        scratch_shapes=[pltpu.VMEM((4 * HALO, rows), F32)] * 4
        + [
            pltpu.VMEM((3 * HALO, wide), F32),
            pltpu.VMEM((4 * HALO, wide), F32),
            pltpu.VMEM((4 * HALO, wide), F32),
            pltpu.VMEM((3 * HALO, wide), F32),
            pltpu.SemaphoreType.DMA((4,)),
            pltpu.SemaphoreType.DMA((4,)),
        ],
        compiler_params=pltpu.CompilerParams(collective_id=0, has_side_effects=True),
        name="halo",
    )(*fields, *fields, *fields, *fields, wave)


CHUNK = 24


def window_kernel(
    n_sect, state, previous, coefficient, stiffness, sides, wave, above, below,
    state_out, previous_out, trace_out, first, second, coef,
):
    rows, lanes = state.shape
    wide = lanes + TILE
    full = rows + 2 * HALO
    s = lax.axis_index("sect")
    on_shell = s == n_sect - 1
    for a, (ref, center) in enumerate(((first, state), (second, previous), (coef, coefficient))):
        part = pl.ds(a * HALO, HALO)
        ref[:HALO] = above[part]
        ref[HALO + rows :] = below[part]
        ref[HALO : HALO + rows, :lanes] = center[...]
        ref[HALO : HALO + rows, lanes:] = sides[a]
    substeps = wave.shape[0]
    shell_scale = jnp.where(on_shell, 1.0, 0.0).astype(F32)
    fluid_scale = 1.0 - shell_scale
    elem_blocks, elem = stiffness.shape[0], stiffness.shape[1]

    def step(k, cur, other):
        for start in range(0, full, CHUNK):
            stop = min(start + CHUNK, full)
            here = cur[start:stop, :]
            if start == 0:
                up = pltpu.roll(here, 1, 0)
            else:
                up = cur[start - 1 : stop - 1, :]
            if stop == full:
                down = pltpu.roll(here, stop - start - 1, 0)
            else:
                down = cur[start + 1 : stop + 1, :]
            near = (up + down) + pltpu.roll(here, 1, 1) + pltpu.roll(here, wide - 1, 1)
            other[start:stop, :] = (
                2.0 * here - other[start:stop, :] + coef[start:stop, :] * (near - 4.0 * here)
            )
        row = wave[pl.ds(k, 1), :]
        up_row = above[pl.ds(3 * HALO + k, 1), :]
        other[HALO - 1 : HALO, :] += coef[HALO - 1 : HALO, :] * (up_row * fluid_scale)
        other[HALO : HALO + 1, :] += coef[HALO : HALO + 1, :] * (row * shell_scale)
        at = HALO + rows - 1
        other[at : at + 1, :] += coef[at : at + 1, :] * (row * fluid_scale)

        @pl.when(on_shell)
        def _():
            for b in range(elem_blocks):
                part = slice(HALO + b * elem, HALO + (b + 1) * elem)
                term = jnp.dot(
                    stiffness[b], cur[part, :].astype(BF16), preferred_element_type=F32
                )
                other[part, :] -= coef[part, :] * term

        seen = jnp.where(
            on_shell, other[HALO : HALO + 1, :lanes], other[at : at + 1, :lanes]
        )
        for b in range(lanes // TILE):
            trace_out[b, pl.ds(k, 1), :] = seen[:, b * TILE : (b + 1) * TILE]

    def pair(i, carry):
        step(2 * i, first, second)
        step(2 * i + 1, second, first)
        return carry

    lax.fori_loop(0, substeps // 2, pair, 0)
    state_out[...] = first[HALO : HALO + rows, :lanes]
    previous_out[...] = second[HALO : HALO + rows, :lanes]


def window(state, previous, coefficient, stiffness, sides, wave, above, below, n_sect):
    rows, lanes = state.shape
    substeps = wave.shape[0]
    return pl.pallas_call(
        functools.partial(window_kernel, n_sect),
        out_shape=(
            jax.ShapeDtypeStruct((rows, lanes), F32),
            jax.ShapeDtypeStruct((rows, lanes), F32),
            jax.ShapeDtypeStruct((lanes // TILE, substeps, TILE), F32),
        ),
        in_specs=[pl.BlockSpec(memory_space=pltpu.VMEM)] * 8,
        out_specs=(pl.BlockSpec(memory_space=pltpu.VMEM),) * 3,
        scratch_shapes=[pltpu.VMEM((rows + 2 * HALO, lanes + TILE), F32)] * 3,
        compiler_params=pltpu.CompilerParams(vmem_limit_bytes=40 * 1024 * 1024),
        name="window",
    )(state, previous, coefficient, stiffness, sides, wave, above, below)


def split(value):
    high = value.astype(BF16)
    low = (value - high.astype(F32)).astype(BF16)
    return high, low


def three_products(x, w, contract):
    x_high, x_low = split(x)
    w_high, w_low = split(w)
    dims = (((1,), (contract,)), ((), ()))
    out = lax.dot_general(x_high, w_high, dims, preferred_element_type=F32)
    out += lax.dot_general(x_low, w_high, dims, preferred_element_type=F32)
    out += lax.dot_general(x_high, w_low, dims, preferred_element_type=F32)
    return out


def push_kernel(n_sect, face, owner, node, trace, rbf, out, terms):
    entries = rbf.shape[0]
    blocks = trace.shape[0]

    @pl.when(lax.axis_index("sect") < n_sect - 1)
    def _():
        out[...] = jnp.zeros_like(out)
        for e in range(entries):
            terms[e] = three_products(trace[face[e]], rbf[e], 0)
        for e in range(entries):
            slot = owner[e] * blocks + node[e]
            out[slot] += terms[e]


def push(face, owner, node, trace, rbf, n_sect, n_dom):
    blocks, substeps, size = trace.shape
    return pl.pallas_call(
        functools.partial(push_kernel, n_sect),
        out_shape=jax.ShapeDtypeStruct((n_dom * blocks, substeps, size), F32),
        in_specs=[pl.BlockSpec(memory_space=pltpu.SMEM)] * 3
        + [pl.BlockSpec(memory_space=pltpu.VMEM)] * 2,
        out_specs=pl.BlockSpec(memory_space=pltpu.VMEM),
        scratch_shapes=[pltpu.VMEM((rbf.shape[0], substeps, size), F32)],
        name="push",
    )(face, owner, node, trace, rbf)


def swap_kernel(
    n_sect, n_dom, outgoing, trace, loads_out, nodes_out,
    arrived, total, parts, nodes, shell_trace,
    load_send, load_recv, part_send, part_recv, down_send, down_recv, node_send, node_recv,
):
    s = lax.axis_index("sect")
    d = lax.axis_index("dom")
    blocks = trace.shape[0]
    shell = n_sect - 1
    on_shell = s == shell
    barrier = pltpu.get_barrier_semaphore()

    @pl.when(on_shell)
    def _():
        for t in range(shell):
            signal(barrier, t, d)
        pl.semaphore_wait(barrier, shell)

    @pl.when(jnp.logical_not(on_shell))
    def _():
        for j in range(1, n_dom):
            signal(barrier, s, lax.rem(d + j, n_dom))
        signal(barrier, shell, d)
        pl.semaphore_wait(barrier, n_dom)

    @pl.when(on_shell)
    def _():
        copies = []
        for t in range(shell):
            copy = remote(trace, shell_trace, down_send.at[t], down_recv, t, d)
            copy.start()
            copies.append(copy)
        nodes_out[...] = jnp.zeros_like(nodes_out)
        for t in range(shell):
            remote(total, parts.at[t], part_send, part_recv.at[t], t, d).wait_recv()
        loads = parts[0]
        for t in range(1, shell):
            loads = loads + parts[t]
        loads_out[...] = loads
        for copy in copies:
            copy.wait_send()

    @pl.when(jnp.logical_not(on_shell))
    def _():
        loads = []
        for j in range(1, n_dom):
            to = lax.rem(d + j, n_dom)
            copy = remote(
                outgoing.at[pl.ds(to * blocks, blocks)], arrived.at[j - 1],
                load_send.at[j - 1], load_recv.at[j - 1], s, to,
            )
            copy.start()
            loads.append(copy)
        value = outgoing[pl.ds(d * blocks, blocks)]
        for j in range(1, n_dom):
            loads[j - 1].wait_recv()
            value = value + arrived[j - 1]
        total[...] = value
        up = remote(total, parts.at[s], part_send, part_recv.at[s], shell, d)
        up.start()
        remote(trace, shell_trace, down_send.at[0], down_recv, shell, d).wait_recv()
        sends = []
        for j in range(1, n_dom):
            to = lax.rem(d + j, n_dom)
            copy = remote(
                shell_trace, nodes.at[j - 1], node_send.at[j - 1], node_recv.at[j - 1], s, to
            )
            copy.start()
            sends.append(copy)
        loads_out[...] = jnp.zeros_like(loads_out)
        nodes_out[0] = shell_trace[...]
        for j in range(1, n_dom):
            sends[j - 1].wait_recv()
            nodes_out[j] = nodes[j - 1]
        for copy in loads + sends + [up]:
            copy.wait_send()


def swap(outgoing, trace, n_sect, n_dom):
    block = trace.shape
    dma = pltpu.SemaphoreType.DMA
    return pl.pallas_call(
        functools.partial(swap_kernel, n_sect, n_dom),
        out_shape=(
            jax.ShapeDtypeStruct(block, F32),
            jax.ShapeDtypeStruct((n_dom,) + block, F32),
        ),
        in_specs=[pl.BlockSpec(memory_space=pltpu.VMEM)] * 2,
        out_specs=(pl.BlockSpec(memory_space=pltpu.VMEM),) * 2,
        scratch_shapes=[
            pltpu.VMEM((n_dom - 1,) + block, F32),
            pltpu.VMEM(block, F32),
            pltpu.VMEM((n_sect - 1,) + block, F32),
            pltpu.VMEM((n_dom - 1,) + block, F32),
            pltpu.VMEM(block, F32),
            dma((n_dom - 1,)),
            dma((n_dom - 1,)),
            dma,
            dma((n_sect - 1,)),
            dma((n_sect - 1,)),
            dma,
            dma((n_dom - 1,)),
            dma((n_dom - 1,)),
        ],
        compiler_params=pltpu.CompilerParams(collective_id=1, has_side_effects=True),
        name="swap",
    )(outgoing, trace)


def pull_kernel(n_sect, n_dom, face, owner, node, loads, nodes, rbf, out, terms, sums):
    entries = rbf.shape[0]
    blocks = loads.shape[0]
    d = lax.axis_index("dom")
    on_shell = lax.axis_index("sect") == n_sect - 1

    @pl.when(on_shell)
    def _():
        for b in range(blocks):
            out[:, b * TILE : (b + 1) * TILE] = loads[b]

    @pl.when(jnp.logical_not(on_shell))
    def _():
        sums[...] = jnp.zeros_like(sums)
        for e in range(entries):
            slot = lax.rem(d - owner[e] + n_dom, n_dom)
            terms[e] = three_products(nodes[slot, node[e]], rbf[e], 1)
        for e in range(entries):
            sums[face[e]] += terms[e]
        for b in range(blocks):
            out[:, b * TILE : (b + 1) * TILE] = sums[b]


def pull(face, owner, node, loads, nodes, rbf, n_sect, n_dom):
    blocks, substeps, size = loads.shape
    return pl.pallas_call(
        functools.partial(pull_kernel, n_sect, n_dom),
        out_shape=jax.ShapeDtypeStruct((substeps, blocks * size), F32),
        in_specs=[pl.BlockSpec(memory_space=pltpu.SMEM)] * 3
        + [pl.BlockSpec(memory_space=pltpu.VMEM)] * 3,
        out_specs=pl.BlockSpec(memory_space=pltpu.VMEM),
        scratch_shapes=[
            pltpu.VMEM((rbf.shape[0], substeps, size), F32),
            pltpu.VMEM((blocks, substeps, size), F32),
        ],
        name="pull",
    )(face, owner, node, loads, nodes, rbf)


def local(
    state, previous, coefficient, stiffness, waveform, entry_face, entry_owner, entry_node, rbf
):
    n_sect = lax.axis_size("sect")
    n_dom = lax.axis_size("dom")
    owner = entry_owner[:, 0]
    wave = waveform[:, 0, :]
    sides, wide_wave, above, below = exchange(state, previous, coefficient, wave, n_sect, n_dom)
    current, before, trace = window(
        state, previous, coefficient, stiffness, sides, wide_wave, above, below, n_sect
    )
    outgoing = push(entry_face, owner, entry_node, trace, rbf, n_sect, n_dom)
    loads, nodes = swap(outgoing, trace, n_sect, n_dom)
    out = pull(entry_face, owner, entry_node, loads, nodes, rbf, n_sect, n_dom)
    return (current, before, out[:, None, :])


def solution(mesh):
    in_specs = (
        P("sect", "dom"),
        P("sect", "dom"),
        P("sect", "dom"),
        P(),
        P(None, ("sect", "dom"), None),
        P(("sect", "dom")),
        P(("sect", "dom"), None),
        P(("sect", "dom")),
        P(("sect", "dom"), None, None),
    )
    out_specs = (P("sect", "dom"), P("sect", "dom"), P(None, ("sect", "dom"), None))
    return jax.shard_map(local, mesh=mesh, in_specs=in_specs, out_specs=out_specs, check_vma=False)
```

time: 254 us -> 49.7 us (0.20)
  starting transfers between devices: 132 us -> 0 us
  other arithmetic: 41.8 us -> 0 us
  Pallas kernels: 0 us -> 41.7 us
  blocking collectives: 27.9 us -> 0 us
  local copies, waits for them, and re-layouts: 26.7 us -> 6.85 us
  waiting for transfers between devices: 15.7 us -> 0 us
  matrix products: 7.01 us -> 0 us
    ppermute x32 -> x0, starting transfers between devices: 110 us -> none  [the longest x16 89.7 us: padded_2(): lax.ppermute(lax.slice_in_dim(block, block.shape[dim] - width, None, axis...]
    pallas_call x0 -> x5, Pallas kernels: none -> 41.7 us  [the longest x1 13.8 us: swap(): pl.pallas_call(functools.partial(swap_kernel, n_sect, n_dom), out_shape=(...]
    add x9 -> x0, other arithmetic: 29.2 us -> none  [the longest x8 28.6 us: local(): 2.0 * current - before + coefficient * (laplace - element_term + source)]
    all_to_all x2 -> x0, starting transfers between devices: 21.4 us -> none  [the longest x1 17.2 us: local(): lax.all_to_all(outgoing.reshape(n_dom, capacity, substeps, block_size), '...]
    psum x1 -> x0, blocking collectives: 18.6 us -> none  [local(): node_loads = lax.psum(partial_loads, 'sect')]
    slice x10 -> x0, local copies, waits for them, and re-layouts: 14.5 us -> none  [the longest x8 13.6 us: local(): padded[2:-1, 1:-1]]
    slice x8 -> x0, other arithmetic: 10.1 us -> none  [padded_2(): lax.slice_in_dim(block, block.shape[dim] - width, None, axis=dim)]
    all_to_all x1 -> x0, blocking collectives: 9.35 us -> none  [local(): lax.all_to_all(replies.reshape(n_dom, capacity, substeps, block_size), 'd...]
  transfers between devices with their start and end apart: 34 -> 0, of which waited for: 9 -> 0; matrix products, arithmetic and copies ran while one was open for 27% -> 0% of each run, Pallas kernels for 0% -> 0%
where the time goes in v1:
time: 49.7 us; the launch traced here: 49.3 us
  Pallas kernels  41.7 us (84%)
  local copies, waits for them, and re-layouts  6.85 us (14%)
  between operations  0.7 us (1%)
    pallas_call x1, Pallas kernels, swap(): pl.pallas_call(functools.partial(swap_kernel, n_sect, n_dom), out_shape=(...  13.8 us
    pallas_call x1, Pallas kernels, exchange(): pl.pallas_call(functools.partial(halo_kernel, n_sect, n_dom), grid=(1,),...  10.7 us
    pallas_call x1, Pallas kernels, window(): pl.pallas_call(functools.partial(window_kernel, n_sect), out_shape=(jax.S...  9.89 us
    unnamed x20, local copies, waits for them, and re-layouts  6.85 us
    pallas_call x1, Pallas kernels, pull(): pl.pallas_call(functools.partial(pull_kernel, n_sect, n_dom), out_shape=j...  4.08 us
    pallas_call x1, Pallas kernels, push(): pl.pallas_call(functools.partial(push_kernel, n_sect), out_shape=jax.Shap...  3.22 us

profile of v1, /device:TPU:0, one launch (start us, length us, event | category | flops | bytes accessed | tf_op | source)
XLA Modules:
  0.0 49.3 jit_solution(5517001285440043307)
XLA Ops:
  0.6 1.3 %copy.15 = f32[8,1,512]{2,0,1:T(8,128)} copy(f32[8,1,512]{2,1,0:T(1,128)} %param.13) | data formatting | bytes 32768
  2.0 0.0 copy-start.1
  2.0 0.0 copy-start.2
  2.0 0.0 copy-start.4
  2.0 10.7 %halo.1 = (f32[3,512,128]{2,1,0:T(8,128)}, f32[8,640]{1,0:T(8,128)}, f32[32,640]{1,0:T(8,128)}, f32[24,640]{1,0:T(8,128)}) custom-call(f32[512,512]{1,0:T(8,128)} %state.1, f32[512,512]{1,0:T(8,128)} %previous.1, f32[512,512]{1,0:T(8,128)} %coefficient.1, f32[512,512]{1,0:T(8,128)} %state.1, f32[512,512]{1,0:T(8,128)} %previous.1, f32[512,512]{1,0:T(8,128)} %coefficient.1, ...), custom_call_target="tpu_custom_call" | custom-call | tf_op jit(solution)/shard_map/halo/pallas_call | solution.py:183
  12.7 0.0 copy-done
  12.7 0.0 copy-done.1
  12.7 0.0 copy-done.2
  12.7 0.0 copy-done.4
  12.7 0.0 copy-start.3
  12.7 1.1 %copy-done.3 = f32[3,512,128]{2,1,0:T(8,128)S(1)} copy-done((f32[3,512,128]{2,1,0:T(8,128)S(1)}, f32[3,512,128]{2,1,0:T(8,128)}, u32[]{:S(2)}) %copy-start.3) | copy-done | bytes 786456
  13.9 0.0 copy-start.5
  13.9 0.9 %copy-done.5 = f32[32,640]{1,0:T(8,128)S(1)} copy-done((f32[32,640]{1,0:T(8,128)S(1)}, f32[32,640]{1,0:T(8,128)}, u32[]{:S(2)}) %copy-start.5) | copy-done | bytes 81944
  14.8 0.0 copy-start.7
  14.8 0.8 %copy-done.7 = f32[24,640]{1,0:T(8,128)S(1)} copy-done((f32[24,640]{1,0:T(8,128)S(1)}, f32[24,640]{1,0:T(8,128)}, u32[]{:S(2)}) %copy-start.7) | copy-done | bytes 61464
  15.6 0.0 copy-start.8
  15.6 0.7 %copy-done.8 = f32[8,640]{1,0:T(8,128)S(1)} copy-done((f32[8,640]{1,0:T(8,128)S(1)}, f32[8,640]{1,0:T(8,128)}, u32[]{:S(2)}) %copy-start.8) | copy-done | bytes 20504
  16.3 9.9 %window.1 = (f32[512,512]{1,0:T(8,128)}, f32[512,512]{1,0:T(8,128)}, f32[4,8,128]{2,1,0:T(8,128)S(1)}) custom-call(f32[512,512]{1,0:T(8,128)S(1)} %copy-done, f32[512,512]{1,0:T(8,128)S(1)} %copy-done.1, f32[512,512]{1,0:T(8,128)S(1)} %copy-done.2, bf16[4,128,128]{2,1,0:T(8,128)(2,1)S(1)} %copy-done.4, f32[3,512,128]{2,1,0:T(8,128)S(1)} %copy-done.3, ...), custom_call_target="tpu_custom_call" | custom-call | tf_op jit(solution)/shard_map/window/pallas_call | solution.py:291
  26.2 0.0 copy-start.6
  26.2 0.6 %copy-done.6 = f32[4,8,128]{2,1,0:T(8,128)} copy-done((f32[4,8,128]{2,1,0:T(8,128)}, f32[4,8,128]{2,1,0:T(8,128)S(1)}, u32[]{:S(2)}) %copy-start.6) | copy-done | bytes 16408
  26.8 3.2 %push.1.outgoing = f32[32,8,128]{2,1,0:T(8,128)} custom-call(s32[32]{0:T(128)} %face.3, s32[32]{0:T(128)} %bitcast.7, s32[32]{0:T(128)} %node.3, f32[4,8,128]{2,1,0:T(8,128)} %copy-done.6, f32[32,128,128]{2,1,0:T(8,128)} %rbf.3), custom_call_target="tpu_custom_call" | custom-call | tf_op jit(solution)/shard_map/push/pallas_call | solution.py:338
  30.0 13.8 %swap.1 = (f32[4,8,128]{2,1,0:T(8,128)}, f32[8,4,8,128]{3,2,1,0:T(8,128)}) custom-call(f32[32,8,128]{2,1,0:T(8,128)} %push.1.outgoing, f32[4,8,128]{2,1,0:T(8,128)} %copy-done.6), custom_call_target="tpu_custom_call" | custom-call | tf_op jit(solution)/shard_map/swap/pallas_call | solution.py:430
  43.8 4.1 %pull.1 = f32[8,512]{1,0:T(8,128)} custom-call(s32[32]{0:T(128)} %face.3, s32[32]{0:T(128)} %bitcast.8, s32[32]{0:T(128)} %node.3, f32[4,8,128]{2,1,0:T(8,128)} %get-tuple-element.19.loads, f32[8,4,8,128]{3,2,1,0:T(8,128)} %get-tuple-element.20.nodes, f32[32,128,128]{2,1,0:T(8,128)} %rbf.3), custom_call_target="tpu_custom_call" | custom-call | tf_op jit(solution)/shard_map/pull/pallas_call | solution.py:483
  47.9 1.3 %copy.12 = f32[8,1,512]{2,1,0:T(1,128)} copy(f32[8,1,512]{2,0,1:T(8,128)} %bitcast.6) | data formatting | bytes 32768
  (1 shorter events, 0.0 us)
Async XLA Ops:
  2.0 10.7 %copy-start = (f32[512,512]{1,0:T(8,128)S(1)}, f32[512,512]{1,0:T(8,128)}, u32[]{:S(2)}) copy-start(f32[512,512]{1,0:T(8,128)} %state.1) | copy-start | bytes 3145732
  2.0 10.8 %copy-start.1 = (f32[512,512]{1,0:T(8,128)S(1)}, f32[512,512]{1,0:T(8,128)}, u32[]{:S(2)}) copy-start(f32[512,512]{1,0:T(8,128)} %previous.1) | copy-start | bytes 3145732
  2.0 10.8 %copy-start.2 = (f32[512,512]{1,0:T(8,128)S(1)}, f32[512,512]{1,0:T(8,128)}, u32[]{:S(2)}) copy-start(f32[512,512]{1,0:T(8,128)} %coefficient.1) | copy-start | bytes 3145732
  2.0 10.8 %copy-start.4 = (bf16[4,128,128]{2,1,0:T(8,128)(2,1)S(1)}, bf16[4,128,128]{2,1,0:T(8,128)(2,1)}, u32[]{:S(2)}) copy-start(bf16[4,128,128]{2,1,0:T(8,128)(2,1)} %stiffness.1) | copy-start | bytes 393220
  12.7 1.1 %copy-start.3 = (f32[3,512,128]{2,1,0:T(8,128)S(1)}, f32[3,512,128]{2,1,0:T(8,128)}, u32[]{:S(2)}) copy-start(f32[3,512,128]{2,1,0:T(8,128)} %get-tuple-element.12.sides) | copy-start | bytes 2359300
  13.9 0.9 %copy-start.5 = (f32[32,640]{1,0:T(8,128)S(1)}, f32[32,640]{1,0:T(8,128)}, u32[]{:S(2)}) copy-start(f32[32,640]{1,0:T(8,128)} %get-tuple-element.14.above) | copy-start | bytes 245764
  14.8 0.8 %copy-start.7 = (f32[24,640]{1,0:T(8,128)S(1)}, f32[24,640]{1,0:T(8,128)}, u32[]{:S(2)}) copy-start(f32[24,640]{1,0:T(8,128)} %get-tuple-element.15.below) | copy-start | bytes 184324
  15.6 0.7 %copy-start.8 = (f32[8,640]{1,0:T(8,128)S(1)}, f32[8,640]{1,0:T(8,128)}, u32[]{:S(2)}) copy-start(f32[8,640]{1,0:T(8,128)} %get-tuple-element.13.wave) | copy-start | bytes 61444
  26.2 0.6 %copy-start.6 = (f32[4,8,128]{2,1,0:T(8,128)}, f32[4,8,128]{2,1,0:T(8,128)S(1)}, u32[]{:S(2)}) copy-start(f32[4,8,128]{2,1,0:T(8,128)S(1)} %get-tuple-element.18.trace) | copy-start | bytes 49156

commit v2 on v1

v2 whole, which is shorter than its diff:
```python
import functools

import jax
import jax.numpy as jnp
from jax import lax
from jax.experimental import pallas as pl
from jax.experimental.pallas import tpu as pltpu
from jax.sharding import PartitionSpec as P

HALO = 8
TILE = 128
F32 = jnp.float32
BF16 = jnp.bfloat16


def signal(barrier, section, column):
    pl.semaphore_signal(
        barrier, inc=1, device_id=(section, column), device_id_type=pl.DeviceIdType.MESH
    )


def remote(source, target, send, recv, section, column):
    return pltpu.make_async_remote_copy(
        src_ref=source,
        dst_ref=target,
        send_sem=send,
        recv_sem=recv,
        device_id=(section, column),
        device_id_type=pl.DeviceIdType.MESH,
    )


def halo_kernel(n_sect, n_dom, *refs):
    fields = refs[0:3]
    wave_ref = refs[3]
    sides_ref, wave_out, above_ref, below_ref = refs[4:8]
    to_left, to_right, from_left, from_right, to_up, to_down, from_up, from_down = refs[8:16]
    from_up_left, from_up_right, from_down_left, from_down_right = refs[16:20]
    send_sem, recv_sem = refs[20:22]
    s = lax.axis_index("sect")
    d = lax.axis_index("dom")
    rows, lanes = fields[0].shape
    substeps = wave_ref.shape[0]
    has_left = d > 0
    has_right = d < n_dom - 1
    has_up = jnp.logical_and(s >= 1, s <= n_sect - 2)
    has_down = s <= n_sect - 3
    both = jnp.logical_and
    first = pl.ds(0, TILE)
    last = pl.ds(lanes - TILE, TILE)
    routes = (
        (has_up, s - 1, d, to_up, from_down, has_down, from_down),
        (has_down, s + 1, d, to_down, from_up, has_up, from_up),
        (has_left, s, d - 1, to_left, from_right, has_right, from_right),
        (has_right, s, d + 1, to_right, from_left, has_left, from_left),
        (both(has_up, has_left), s - 1, d - 1, to_up.at[:, first], from_down_right,
         both(has_down, has_right), from_down_right),
        (both(has_up, has_right), s - 1, d + 1, to_up.at[:, last], from_down_left,
         both(has_down, has_left), from_down_left),
        (both(has_down, has_left), s + 1, d - 1, to_down.at[:, first], from_up_right,
         both(has_up, has_right), from_up_right),
        (both(has_down, has_right), s + 1, d + 1, to_down.at[:, last], from_up_left,
         both(has_up, has_left), from_up_left),
    )
    barrier = pltpu.get_barrier_semaphore()
    for has, section, column, *_ in routes:

        @pl.when(has)
        def _(section=section, column=column):
            signal(barrier, section, column)

    wave = jnp.concatenate([wave_ref[k] for k in range(substeps)], 0)
    for a in range(3):
        part = pl.ds(a * HALO, HALO)
        to_up[part] = fields[a][:HALO]
        to_down[part] = fields[a][rows - HALO :]
    to_down[3 * HALO :] = wave
    lane = lax.broadcasted_iota(jnp.int32, (rows, TILE), 1)

    def pack(where, start):
        a = fields[0][:, where]
        b = pltpu.roll(fields[1][:, where], (HALO - start) % TILE, 1)
        c = pltpu.roll(fields[2][:, where], (2 * HALO - start) % TILE, 1)
        if start:
            a = pltpu.roll(a, TILE - start, 1)
        packed = jnp.where(lane < HALO, a, jnp.where(lane < 2 * HALO, b, c))
        return packed.T[: 3 * HALO]

    to_left[: 3 * HALO] = pack(first, 0)
    to_left[3 * HALO :, :TILE] = wave[:, :TILE]
    to_left[3 * HALO :, TILE:] = jnp.zeros((HALO, rows - TILE), F32)
    to_right[: 3 * HALO] = pack(last, TILE - HALO)
    to_right[3 * HALO :, :TILE] = wave[:, lanes - TILE :]
    to_right[3 * HALO :, TILE:] = jnp.zeros((HALO, rows - TILE), F32)

    peers = sum(jnp.where(route[0], 1, 0).astype(jnp.int32) for route in routes)
    pl.semaphore_wait(barrier, peers)

    copies = []
    for i, (has, section, column, source, target, _, _) in enumerate(routes):
        copy = remote(source, target, send_sem.at[i], recv_sem.at[i], section, column)
        copies.append(copy)

        @pl.when(has)
        def _(copy=copy):
            copy.start()

    wave_out[:, :lanes] = wave
    for i in (2, 3, 0, 1, 4, 5, 6, 7):
        comes, buf = routes[i][5:]

        @pl.when(comes)
        def _(copy=copies[i]):
            copy.wait_recv()

        @pl.when(jnp.logical_not(comes))
        def _(buf=buf):
            buf[...] = jnp.zeros_like(buf)

        if i == 3:
            fill = jnp.zeros((TILE - 3 * HALO, rows), F32)
            right = jnp.concatenate([from_right[: 3 * HALO], fill], 0).T
            left = jnp.concatenate([from_left[: 3 * HALO], fill], 0).T
            for a in range(3):
                r = pltpu.roll(right, (TILE - a * HALO) % TILE, 1) if a else right
                le = pltpu.roll(left, TILE - (a + 1) * HALO, 1)
                sides_ref[a] = jnp.where(
                    lane < HALO, r, jnp.where(lane >= TILE - HALO, le, 0.0)
                )

    def join(right_part, left_part):
        at = lax.broadcasted_iota(jnp.int32, right_part.shape, 1)
        return jnp.where(at < HALO, right_part, jnp.where(at >= TILE - HALO, left_part, 0.0))

    wave_out[:, lanes:] = join(from_right[3 * HALO :, :TILE], from_left[3 * HALO :, :TILE])
    above_ref[:, :lanes] = from_up[...]
    above_ref[:, lanes:] = join(from_up_right[...], from_up_left[...])
    below_ref[:, :lanes] = from_down[...]
    below_ref[:, lanes:] = join(from_down_right[...], from_down_left[...])

    for route, copy in zip(routes, copies):

        @pl.when(route[0])
        def _(copy=copy):
            copy.wait_send()


def exchange(state, previous, coefficient, wave, n_sect, n_dom):
    rows, lanes = state.shape
    wide = lanes + TILE
    vmem = pl.BlockSpec(memory_space=pltpu.VMEM)
    return pl.pallas_call(
        functools.partial(halo_kernel, n_sect, n_dom),
        out_shape=(
            jax.ShapeDtypeStruct((3, rows, TILE), F32),
            jax.ShapeDtypeStruct((HALO, wide), F32),
            jax.ShapeDtypeStruct((4 * HALO, wide), F32),
            jax.ShapeDtypeStruct((3 * HALO, wide), F32),
        ),
        in_specs=[vmem] * 4,
        out_specs=(vmem,) * 4,
        scratch_shapes=[pltpu.VMEM((4 * HALO, rows), F32)] * 4
        + [
            pltpu.VMEM((3 * HALO, lanes), F32),
            pltpu.VMEM((4 * HALO, lanes), F32),
            pltpu.VMEM((4 * HALO, lanes), F32),
            pltpu.VMEM((3 * HALO, lanes), F32),
            pltpu.VMEM((4 * HALO, TILE), F32),
            pltpu.VMEM((4 * HALO, TILE), F32),
            pltpu.VMEM((3 * HALO, TILE), F32),
            pltpu.VMEM((3 * HALO, TILE), F32),
            pltpu.SemaphoreType.DMA((8,)),
            pltpu.SemaphoreType.DMA((8,)),
        ],
        compiler_params=pltpu.CompilerParams(collective_id=0, has_side_effects=True),
        name="halo",
    )(state, previous, coefficient, wave)


CHUNK = 24


def window_kernel(
    n_sect, face, owner, node, state, previous, coefficient, stiffness, sides, wave, above,
    below, rbf, state_out, previous_out, trace_out, slots, high, low, first, second, coef, terms,
):
    rows, lanes = state.shape
    wide = lanes + TILE
    full = rows + 2 * HALO
    s = lax.axis_index("sect")
    on_shell = s == n_sect - 1
    for a, (ref, center) in enumerate(((first, state), (second, previous), (coef, coefficient))):
        part = pl.ds(a * HALO, HALO)
        ref[:HALO] = above[part]
        ref[HALO + rows :] = below[part]
        ref[HALO : HALO + rows, :lanes] = center[...]
        ref[HALO : HALO + rows, lanes:] = sides[a]
    substeps = wave.shape[0]
    shell_scale = jnp.where(on_shell, 1.0, 0.0).astype(F32)
    fluid_scale = 1.0 - shell_scale
    elem_blocks, elem = stiffness.shape[0], stiffness.shape[1]

    def step(k, cur, other):
        for start in range(0, full, CHUNK):
            stop = min(start + CHUNK, full)
            here = cur[start:stop, :]
            if start == 0:
                up = pltpu.roll(here, 1, 0)
            else:
                up = cur[start - 1 : stop - 1, :]
            if stop == full:
                down = pltpu.roll(here, stop - start - 1, 0)
            else:
                down = cur[start + 1 : stop + 1, :]
            near = (up + down) + pltpu.roll(here, 1, 1) + pltpu.roll(here, wide - 1, 1)
            other[start:stop, :] = (
                2.0 * here - other[start:stop, :] + coef[start:stop, :] * (near - 4.0 * here)
            )
        row = wave[pl.ds(k, 1), :]
        up_row = above[pl.ds(3 * HALO + k, 1), :]
        other[HALO - 1 : HALO, :] += coef[HALO - 1 : HALO, :] * (up_row * fluid_scale)
        other[HALO : HALO + 1, :] += coef[HALO : HALO + 1, :] * (row * shell_scale)
        at = HALO + rows - 1
        other[at : at + 1, :] += coef[at : at + 1, :] * (row * fluid_scale)

        @pl.when(on_shell)
        def _():
            for b in range(elem_blocks):
                part = slice(HALO + b * elem, HALO + (b + 1) * elem)
                term = jnp.dot(
                    stiffness[b], cur[part, :].astype(BF16), preferred_element_type=F32
                )
                other[part, :] -= coef[part, :] * term

        seen = jnp.where(
            on_shell, other[HALO : HALO + 1, :lanes], other[at : at + 1, :lanes]
        )
        for b in range(lanes // TILE):
            trace_out[b, pl.ds(k, 1), :] = seen[:, b * TILE : (b + 1) * TILE]

    def pair(i, carry):
        step(2 * i, first, second)
        step(2 * i + 1, second, first)
        return carry

    lax.fori_loop(0, substeps // 2, pair, 0)
    state_out[...] = first[HALO : HALO + rows, :lanes]
    previous_out[...] = second[HALO : HALO + rows, :lanes]


    entries = rbf.shape[0]
    blocks = trace_out.shape[0]

    @pl.when(jnp.logical_not(on_shell))
    def _():
        slots[...] = jnp.zeros_like(slots)
        for e in range(entries):
            w_high, w_low = split(rbf[e])
            high[e] = w_high
            low[e] = w_low
            terms[e] = three_products(trace_out[face[e]], w_high, w_low, 0)
        for e in range(entries):
            slots[owner[e, 0] * blocks + node[e]] += terms[e]


def window(
    face, owner, node, state, previous, coefficient, stiffness, sides, wave, above, below, rbf,
    n_sect, n_dom,
):
    rows, lanes = state.shape
    substeps = wave.shape[0]
    blocks = lanes // TILE
    vmem = pl.BlockSpec(memory_space=pltpu.VMEM)
    return pl.pallas_call(
        functools.partial(window_kernel, n_sect),
        out_shape=(
            jax.ShapeDtypeStruct((rows, lanes), F32),
            jax.ShapeDtypeStruct((rows, lanes), F32),
            jax.ShapeDtypeStruct((blocks, substeps, TILE), F32),
            jax.ShapeDtypeStruct((n_dom * blocks, substeps, TILE), F32),
            jax.ShapeDtypeStruct(rbf.shape, BF16),
            jax.ShapeDtypeStruct(rbf.shape, BF16),
        ),
        in_specs=[pl.BlockSpec(memory_space=pltpu.SMEM)] * 3 + [vmem] * 9,
        out_specs=(vmem,) * 6,
        scratch_shapes=[pltpu.VMEM((rows + 2 * HALO, lanes + TILE), F32)] * 3
        + [pltpu.VMEM((rbf.shape[0], substeps, TILE), F32)],
        compiler_params=pltpu.CompilerParams(vmem_limit_bytes=40 * 1024 * 1024),
        name="window",
    )(
        face, owner, node, state, previous, coefficient, stiffness, sides, wave, above, below,
        rbf,
    )


def split(value):
    high = value.astype(BF16)
    low = (value - high.astype(F32)).astype(BF16)
    return high, low


def three_products(x, w_high, w_low, contract):
    x_high, x_low = split(x)
    dims = (((1,), (contract,)), ((), ()))
    out = lax.dot_general(x_high, w_high, dims, preferred_element_type=F32)
    out += lax.dot_general(x_low, w_high, dims, preferred_element_type=F32)
    out += lax.dot_general(x_high, w_low, dims, preferred_element_type=F32)
    return out


def swap_kernel(
    n_sect, n_dom, outgoing, trace, loads_out, nodes_out,
    arrived, total, parts, nodes, shell_trace,
    load_send, load_recv, part_send, part_recv, down_send, down_recv, node_send, node_recv,
):
    s = lax.axis_index("sect")
    d = lax.axis_index("dom")
    blocks = trace.shape[0]
    shell = n_sect - 1
    on_shell = s == shell
    barrier = pltpu.get_barrier_semaphore()

    @pl.when(on_shell)
    def _():
        for t in range(shell):
            signal(barrier, t, d)
        pl.semaphore_wait(barrier, shell)

    @pl.when(jnp.logical_not(on_shell))
    def _():
        for j in range(1, n_dom):
            signal(barrier, s, lax.rem(d + j, n_dom))
        signal(barrier, shell, d)
        pl.semaphore_wait(barrier, n_dom)

    @pl.when(on_shell)
    def _():
        copies = []
        for t in range(shell):
            copy = remote(trace, shell_trace, down_send.at[t], down_recv, t, d)
            copy.start()
            copies.append(copy)
        nodes_out[...] = jnp.zeros_like(nodes_out)
        for t in range(shell):
            remote(total, parts.at[t], part_send, part_recv.at[t], t, d).wait_recv()
        loads = parts[0]
        for t in range(1, shell):
            loads = loads + parts[t]
        loads_out[...] = loads
        for copy in copies:
            copy.wait_send()

    @pl.when(jnp.logical_not(on_shell))
    def _():
        loads = []
        for j in range(1, n_dom):
            to = lax.rem(d + j, n_dom)
            copy = remote(
                outgoing.at[pl.ds(to * blocks, blocks)], arrived.at[j - 1],
                load_send.at[j - 1], load_recv.at[j - 1], s, to,
            )
            copy.start()
            loads.append(copy)
        remote(trace, shell_trace, down_send.at[0], down_recv, shell, d).wait_recv()
        sends = []
        for j in range(1, n_dom):
            to = lax.rem(d + j, n_dom)
            copy = remote(
                shell_trace, nodes.at[j - 1], node_send.at[j - 1], node_recv.at[j - 1], s, to
            )
            copy.start()
            sends.append(copy)
        value = outgoing[pl.ds(d * blocks, blocks)]
        for j in range(1, n_dom):
            loads[j - 1].wait_recv()
            value = value + arrived[j - 1]
        total[...] = value
        up = remote(total, parts.at[s], part_send, part_recv.at[s], shell, d)
        up.start()
        loads_out[...] = jnp.zeros_like(loads_out)
        nodes_out[0] = shell_trace[...]
        for j in range(1, n_dom):
            sends[j - 1].wait_recv()
            nodes_out[j] = nodes[j - 1]
        for copy in loads + sends + [up]:
            copy.wait_send()


def swap(outgoing, trace, n_sect, n_dom):
    block = trace.shape
    dma = pltpu.SemaphoreType.DMA
    return pl.pallas_call(
        functools.partial(swap_kernel, n_sect, n_dom),
        out_shape=(
            jax.ShapeDtypeStruct(block, F32),
            jax.ShapeDtypeStruct((n_dom,) + block, F32),
        ),
        in_specs=[pl.BlockSpec(memory_space=pltpu.VMEM)] * 2,
        out_specs=(pl.BlockSpec(memory_space=pltpu.VMEM),) * 2,
        scratch_shapes=[
            pltpu.VMEM((n_dom - 1,) + block, F32),
            pltpu.VMEM(block, F32),
            pltpu.VMEM((n_sect - 1,) + block, F32),
            pltpu.VMEM((n_dom - 1,) + block, F32),
            pltpu.VMEM(block, F32),
            dma((n_dom - 1,)),
            dma((n_dom - 1,)),
            dma,
            dma((n_sect - 1,)),
            dma((n_sect - 1,)),
            dma,
            dma((n_dom - 1,)),
            dma((n_dom - 1,)),
        ],
        compiler_params=pltpu.CompilerParams(collective_id=1, has_side_effects=True),
        name="swap",
    )(outgoing, trace)


def pull_kernel(n_sect, n_dom, face, owner, node, loads, nodes, high, low, out, terms, sums):
    entries = high.shape[0]
    substeps = out.shape[0]
    blocks = loads.shape[0]
    d = lax.axis_index("dom")
    on_shell = lax.axis_index("sect") == n_sect - 1

    @pl.when(on_shell)
    def _():
        for b in range(blocks):
            for k in range(substeps):
                out[k, :, b * TILE : (b + 1) * TILE] = loads[b, k : k + 1, :]

    @pl.when(jnp.logical_not(on_shell))
    def _():
        sums[...] = jnp.zeros_like(sums)
        for e in range(entries):
            slot = lax.rem(d - owner[e, 0] + n_dom, n_dom)
            terms[e] = three_products(nodes[slot, node[e]], high[e], low[e], 1)
        for e in range(entries):
            sums[face[e]] += terms[e]
        for b in range(blocks):
            for k in range(substeps):
                out[k, :, b * TILE : (b + 1) * TILE] = sums[b, k : k + 1, :]


def pull(face, owner, node, loads, nodes, high, low, n_sect, n_dom):
    blocks, substeps, size = loads.shape
    return pl.pallas_call(
        functools.partial(pull_kernel, n_sect, n_dom),
        out_shape=jax.ShapeDtypeStruct((substeps, 1, blocks * size), F32),
        in_specs=[pl.BlockSpec(memory_space=pltpu.SMEM)] * 3
        + [pl.BlockSpec(memory_space=pltpu.VMEM)] * 4,
        out_specs=pl.BlockSpec(memory_space=pltpu.VMEM),
        scratch_shapes=[
            pltpu.VMEM((high.shape[0], substeps, size), F32),
            pltpu.VMEM((blocks, substeps, size), F32),
        ],
        name="pull",
    )(face, owner, node, loads, nodes, high, low)


def local(
    state, previous, coefficient, stiffness, waveform, entry_face, entry_owner, entry_node, rbf
):
    n_sect = lax.axis_size("sect")
    n_dom = lax.axis_size("dom")
    sides, wave, above, below = exchange(state, previous, coefficient, waveform, n_sect, n_dom)
    current, before, trace, outgoing, high, low = window(
        entry_face, entry_owner, entry_node, state, previous, coefficient, stiffness, sides,
        wave, above, below, rbf, n_sect, n_dom,
    )
    loads, nodes = swap(outgoing, trace, n_sect, n_dom)
    out = pull(entry_face, entry_owner, entry_node, loads, nodes, high, low, n_sect, n_dom)
    return (current, before, out)


def solution(mesh):
    in_specs = (
        P("sect", "dom"),
        P("sect", "dom"),
        P("sect", "dom"),
        P(),
        P(None, ("sect", "dom"), None),
        P(("sect", "dom")),
        P(("sect", "dom"), None),
        P(("sect", "dom")),
        P(("sect", "dom"), None, None),
    )
    out_specs = (P("sect", "dom"), P("sect", "dom"), P(None, ("sect", "dom"), None))
    return jax.shard_map(local, mesh=mesh, in_specs=in_specs, out_specs=out_specs, check_vma=False)
```

time: 49.7 us -> 49.9 us (level)
  local copies, waits for them, and re-layouts: 6.85 us -> 10.2 us
  Pallas kernels: 41.7 us -> 38.5 us
    pallas_call x2 -> x1, Pallas kernels: 13.9 us -> 10.5 us  [exchange(): pl.pallas_call(functools.partial(halo_kernel, n_sect, n_dom), out_shape=(...]
    unnamed x20 -> x33, local copies, waits for them, and re-layouts: 6.85 us -> 10.2 us
    pallas_call x1, Pallas kernels: 9.89 us -> 11.7 us  [window(): pl.pallas_call(functools.partial(window_kernel, n_sect), out_shape=(jax.S...]
    pallas_call x1, Pallas kernels: 13.8 us -> 12.3 us  [swap(): pl.pallas_call(functools.partial(swap_kernel, n_sect, n_dom), out_shape=(...]
where the time goes in v2:
time: 49.9 us; the launch traced here: 49.5 us
  Pallas kernels  38.5 us (77%)
  local copies, waits for them, and re-layouts  10.2 us (20%)
  between operations  0.74 us (1%)
    pallas_call x1, Pallas kernels, swap(): pl.pallas_call(functools.partial(swap_kernel, n_sect, n_dom), out_shape=(...  12.3 us
    pallas_call x1, Pallas kernels, window(): pl.pallas_call(functools.partial(window_kernel, n_sect), out_shape=(jax.S...  11.7 us
    pallas_call x1, Pallas kernels, exchange(): pl.pallas_call(functools.partial(halo_kernel, n_sect, n_dom), out_shape=(...  10.5 us
    unnamed x33, local copies, waits for them, and re-layouts  10.2 us
    pallas_call x1, Pallas kernels, pull(): pl.pallas_call(functools.partial(pull_kernel, n_sect, n_dom), out_shape=j...  4.04 us

profile of v2, /device:TPU:0, one launch (start us, length us, event | category | flops | bytes accessed | tf_op | source)
XLA Modules:
  0.0 49.5 jit_solution(6929168209847079553)
XLA Ops:
  0.6 0.0 copy-start.15
  0.6 0.0 copy-start.14
  0.7 0.0 copy-start.2
  0.7 0.0 copy-start.1
  0.7 0.0 copy-start
  0.7 0.9 %copy.12.owner = s32[32,1]{1,0:T(8,128)S(1)} copy(s32[32,1]{0,1:T(1,128)} %param.15) | data formatting | bytes 256 | tf_op args[6]
  1.6 10.5 %halo.1 = (f32[3,512,128]{2,1,0:T(8,128)}, f32[8,640]{1,0:T(8,128)}, f32[32,640]{1,0:T(8,128)}, f32[24,640]{1,0:T(8,128)}) custom-call(f32[512,512]{1,0:T(8,128)} %state.1, f32[512,512]{1,0:T(8,128)} %previous.1, f32[512,512]{1,0:T(8,128)} %coefficient.1, f32[8,1,512]{2,1,0:T(1,128)} %refs_3_.1), custom_call_target="tpu_custom_call" | custom-call | tf_op jit(solution)/shard_map/halo/pallas_call | solution.py:152
  12.1 0.0 copy-done.15
  12.1 0.0 copy-done.14
  12.1 0.0 copy-start.3
  12.1 1.6 %copy-done.3 = f32[32,128,128]{2,1,0:T(8,128)S(1)} copy-done((f32[32,128,128]{2,1,0:T(8,128)S(1)}, f32[32,128,128]{2,1,0:T(8,128)}, u32[]{:S(2)}) %copy-start.3) | copy-done | bytes 2097176
  13.7 1.1 %copy-done.6 = f32[3,512,128]{2,1,0:T(8,128)S(1)} copy-done((f32[3,512,128]{2,1,0:T(8,128)S(1)}, f32[3,512,128]{2,1,0:T(8,128)}, u32[]{:S(2)}) %copy-start.6) | copy-done | bytes 786456
  14.8 0.9 %copy-done.9 = bf16[4,128,128]{2,1,0:T(8,128)(2,1)S(1)} copy-done((bf16[4,128,128]{2,1,0:T(8,128)(2,1)S(1)}, bf16[4,128,128]{2,1,0:T(8,128)(2,1)}, u32[]{:S(2)}) %copy-start.9) | copy-done | bytes 131096
  15.7 0.9 %copy-done.10 = f32[32,640]{1,0:T(8,128)S(1)} copy-done((f32[32,640]{1,0:T(8,128)S(1)}, f32[32,640]{1,0:T(8,128)}, u32[]{:S(2)}) %copy-start.10) | copy-done | bytes 81944
  16.6 0.8 %copy-done.11 = f32[24,640]{1,0:T(8,128)S(1)} copy-done((f32[24,640]{1,0:T(8,128)S(1)}, f32[24,640]{1,0:T(8,128)}, u32[]{:S(2)}) %copy-start.11) | copy-done | bytes 61464
  17.5 0.7 %copy-done.12 = f32[8,640]{1,0:T(8,128)S(1)} copy-done((f32[8,640]{1,0:T(8,128)S(1)}, f32[8,640]{1,0:T(8,128)}, u32[]{:S(2)}) %copy-start.12) | copy-done | bytes 20504
  18.2 11.7 %window.1 = (f32[512,512]{1,0:T(8,128)}, f32[512,512]{1,0:T(8,128)}, f32[4,8,128]{2,1,0:T(8,128)S(1)}, f32[32,8,128]{2,1,0:T(8,128)S(1)}, bf16[32,128,128]{2,1,0...) custom-call(s32[32]{0:T(128)S(1)} %copy-done.14, s32[32,1]{1,0:T(8,128)S(1)} %copy.12.owner, s32[32]{0:T(128)S(1)} %copy-done.15, ...), custom_call_target="tpu_custom_call" | custom-call | tf_op jit(solution)/shard_map/window/pallas_call | solution.py:274
  29.9 0.0 copy-done.7
  29.9 1.0 %copy-done.4 = bf16[32,128,128]{2,1,0:T(8,128)(2,1)} copy-done((bf16[32,128,128]{2,1,0:T(8,128)(2,1)}, bf16[32,128,128]{2,1,0:T(8,128)(2,1)S(1)}, u32[]{:S(2)}) %copy-start.4) | copy-done | bytes 1048600
  30.9 1.0 %copy-done.5 = bf16[32,128,128]{2,1,0:T(8,128)(2,1)} copy-done((bf16[32,128,128]{2,1,0:T(8,128)(2,1)}, bf16[32,128,128]{2,1,0:T(8,128)(2,1)S(1)}, u32[]{:S(2)}) %copy-start.5) | copy-done | bytes 1048600
  31.9 0.6 %copy-done.8 = f32[32,8,128]{2,1,0:T(8,128)} copy-done((f32[32,8,128]{2,1,0:T(8,128)}, f32[32,8,128]{2,1,0:T(8,128)S(1)}, u32[]{:S(2)}) %copy-start.8) | copy-done | bytes 131096
  32.5 0.6 %copy-done.13 = f32[4,8,128]{2,1,0:T(8,128)} copy-done((f32[4,8,128]{2,1,0:T(8,128)}, f32[4,8,128]{2,1,0:T(8,128)S(1)}, u32[]{:S(2)}) %copy-start.13) | copy-done | bytes 16408
  33.1 12.3 %swap.1 = (f32[4,8,128]{2,1,0:T(8,128)}, f32[8,4,8,128]{3,2,1,0:T(8,128)}) custom-call(f32[32,8,128]{2,1,0:T(8,128)} %copy-done.8, f32[4,8,128]{2,1,0:T(8,128)} %copy-done.13), custom_call_target="tpu_custom_call" | custom-call | tf_op jit(solution)/shard_map/swap/pallas_call | solution.py:392
  45.4 4.0 %pull.1 = f32[8,1,512]{2,1,0:T(1,128)} custom-call(s32[32]{0:T(128)} %face.3, s32[32,1]{1,0:T(8,128)} %copy-done.7, s32[32]{0:T(128)} %node.3, f32[4,8,128]{2,1,0:T(8,128)} %get-tuple-element.23.loads, f32[8,4,8,128]{3,2,1,0:T(8,128)} %get-tuple-element.24.nodes, bf16[32,128,128]{2,1,0:T(8,128)(2,1)} %copy-done.4, bf16[32,128,128]{2,1,0:T(8,128)(2,1)} %copy-done.5), custom_call_target="tpu_custom_call" | custom-call | tf_op jit(solution)/shard_map/pull/pallas_call | solution.py:448
  (13 shorter events, 0.0 us)
Async XLA Ops:
  0.6 11.4 %copy-start.15 = (s32[32]{0:T(128)S(1)}, s32[32]{0:T(128)}, u32[]{:S(2)}) copy-start(s32[32]{0:T(128)} %node.3) | copy-start | bytes 388
  0.6 11.4 %copy-start.14 = (s32[32]{0:T(128)S(1)}, s32[32]{0:T(128)}, u32[]{:S(2)}) copy-start(s32[32]{0:T(128)} %face.3) | copy-start | bytes 388
  0.7 11.4 %copy-start.2 = (f32[512,512]{1,0:T(8,128)S(1)}, f32[512,512]{1,0:T(8,128)}, u32[]{:S(2)}) copy-start(f32[512,512]{1,0:T(8,128)} %coefficient.1) | copy-start | bytes 3145732
  0.7 11.4 %copy-start.1 = (f32[512,512]{1,0:T(8,128)S(1)}, f32[512,512]{1,0:T(8,128)}, u32[]{:S(2)}) copy-start(f32[512,512]{1,0:T(8,128)} %previous.1) | copy-start | bytes 3145732
  0.7 11.4 %copy-start = (f32[512,512]{1,0:T(8,128)S(1)}, f32[512,512]{1,0:T(8,128)}, u32[]{:S(2)}) copy-start(f32[512,512]{1,0:T(8,128)} %state.1) | copy-start | bytes 3145732
  1.6 28.3 %copy-start.7 = (s32[32,1]{1,0:T(8,128)}, s32[32,1]{1,0:T(8,128)S(1)}, u32[]{:S(2)}) copy-start(s32[32,1]{1,0:T(8,128)S(1)} %copy.12.owner) | copy-start | bytes 388
  12.1 1.6 %copy-start.3 = (f32[32,128,128]{2,1,0:T(8,128)S(1)}, f32[32,128,128]{2,1,0:T(8,128)}, u32[]{:S(2)}) copy-start(f32[32,128,128]{2,1,0:T(8,128)} %rbf.1) | copy-start | bytes 6291460
  13.7 1.1 %copy-start.6 = (f32[3,512,128]{2,1,0:T(8,128)S(1)}, f32[3,512,128]{2,1,0:T(8,128)}, u32[]{:S(2)}) copy-start(f32[3,512,128]{2,1,0:T(8,128)} %get-tuple-element.15.sides) | copy-start | bytes 2359300
  14.8 0.9 %copy-start.9 = (bf16[4,128,128]{2,1,0:T(8,128)(2,1)S(1)}, bf16[4,128,128]{2,1,0:T(8,128)(2,1)}, u32[]{:S(2)}) copy-start(bf16[4,128,128]{2,1,0:T(8,128)(2,1)} %stiffness.1) | copy-start | bytes 393220
  15.7 0.9 %copy-start.10 = (f32[32,640]{1,0:T(8,128)S(1)}, f32[32,640]{1,0:T(8,128)}, u32[]{:S(2)}) copy-start(f32[32,640]{1,0:T(8,128)} %get-tuple-element.17.above) | copy-start | bytes 245764
  16.6 0.8 %copy-start.11 = (f32[24,640]{1,0:T(8,128)S(1)}, f32[24,640]{1,0:T(8,128)}, u32[]{:S(2)}) copy-start(f32[24,640]{1,0:T(8,128)} %get-tuple-element.18.below) | copy-start | bytes 184324
  17.5 0.7 %copy-start.12 = (f32[8,640]{1,0:T(8,128)S(1)}, f32[8,640]{1,0:T(8,128)}, u32[]{:S(2)}) copy-start(f32[8,640]{1,0:T(8,128)} %get-tuple-element.16.wave) | copy-start | bytes 61444
  29.9 1.0 %copy-start.4 = (bf16[32,128,128]{2,1,0:T(8,128)(2,1)}, bf16[32,128,128]{2,1,0:T(8,128)(2,1)S(1)}, u32[]{:S(2)}) copy-start(bf16[32,128,128]{2,1,0:T(8,128)(2,1)S(1)} %get-tuple-element.25.high) | copy-start | bytes 3145732
  30.9 1.0 %copy-start.5 = (bf16[32,128,128]{2,1,0:T(8,128)(2,1)}, bf16[32,128,128]{2,1,0:T(8,128)(2,1)S(1)}, u32[]{:S(2)}) copy-start(bf16[32,128,128]{2,1,0:T(8,128)(2,1)S(1)} %get-tuple-element.26.low) | copy-start | bytes 3145732
  31.9 0.7 %copy-start.8 = (f32[32,8,128]{2,1,0:T(8,128)}, f32[32,8,128]{2,1,0:T(8,128)S(1)}, u32[]{:S(2)}) copy-start(f32[32,8,128]{2,1,0:T(8,128)S(1)} %get-tuple-element.21.outgoing) | copy-start | bytes 393220
  32.5 0.6 %copy-start.13 = (f32[4,8,128]{2,1,0:T(8,128)}, f32[4,8,128]{2,1,0:T(8,128)S(1)}, u32[]{:S(2)}) copy-start(f32[4,8,128]{2,1,0:T(8,128)S(1)} %get-tuple-element.22.trace) | copy-start | bytes 49156

commit v3 on v2

--- a/solution.py
+++ b/solution.py
@@ -182,19 +182,38 @@
 
 def window_kernel(
     n_sect, face, owner, node, state, previous, coefficient, stiffness, sides, wave, above,
-    below, rbf, state_out, previous_out, trace_out, slots, high, low, first, second, coef, terms,
+    below, rbf, state_out, previous_out, trace_out, slots, first, second, coef, terms,
+    matrices, wave_own, wave_up, weights, sems,
 ):
     rows, lanes = state.shape
     wide = lanes + TILE
     full = rows + 2 * HALO
     s = lax.axis_index("sect")
     on_shell = s == n_sect - 1
+    inner = pl.ds(HALO, rows)
+    left = pl.ds(0, lanes)
+    moves = [(rbf, weights)]
     for a, (ref, center) in enumerate(((first, state), (second, previous), (coef, coefficient))):
         part = pl.ds(a * HALO, HALO)
-        ref[:HALO] = above[part]
-        ref[HALO + rows :] = below[part]
-        ref[HALO : HALO + rows, :lanes] = center[...]
-        ref[HALO : HALO + rows, lanes:] = sides[a]
+        moves += [
+            (center, ref.at[inner, left]),
+            (sides.at[a], ref.at[inner, pl.ds(lanes, TILE)]),
+            (above.at[part], ref.at[pl.ds(0, HALO)]),
+            (below.at[part], ref.at[pl.ds(HALO + rows, HALO)]),
+        ]
+    moves += [
+        (wave, wave_own),
+        (above.at[pl.ds(3 * HALO, HALO)], wave_up),
+        (stiffness, matrices),
+    ]
+    loads = [
+        pltpu.make_async_copy(source, target, sems.at[i])
+        for i, (source, target) in enumerate(moves)
+    ]
+    for copy in loads[1:] + loads[:1]:
+        copy.start()
+    for copy in loads[1:]:
+        copy.wait()
     substeps = wave.shape[0]
     shell_scale = jnp.where(on_shell, 1.0, 0.0).astype(F32)
     fluid_scale = 1.0 - shell_scale
@@ -216,8 +235,8 @@
             other[start:stop, :] = (
                 2.0 * here - other[start:stop, :] + coef[start:stop, :] * (near - 4.0 * here)
             )
-        row = wave[pl.ds(k, 1), :]
-        up_row = above[pl.ds(3 * HALO + k, 1), :]
+        row = wave_own[pl.ds(k, 1), :]
+        up_row = wave_up[pl.ds(k, 1), :]
         other[HALO - 1 : HALO, :] += coef[HALO - 1 : HALO, :] * (up_row * fluid_scale)
         other[HALO : HALO + 1, :] += coef[HALO : HALO + 1, :] * (row * shell_scale)
         at = HALO + rows - 1
@@ -228,7 +247,7 @@
             for b in range(elem_blocks):
                 part = slice(HALO + b * elem, HALO + (b + 1) * elem)
                 term = jnp.dot(
-                    stiffness[b], cur[part, :].astype(BF16), preferred_element_type=F32
+                    matrices[b], cur[part, :].astype(BF16), preferred_element_type=F32
                 )
                 other[part, :] -= coef[part, :] * term
 
@@ -244,8 +263,13 @@
         return carry
 
     lax.fori_loop(0, substeps // 2, pair, 0)
-    state_out[...] = first[HALO : HALO + rows, :lanes]
-    previous_out[...] = second[HALO : HALO + rows, :lanes]
+    leave = [
+        pltpu.make_async_copy(first.at[inner, left], state_out, sems.at[len(moves)]),
+        pltpu.make_async_copy(second.at[inner, left], previous_out, sems.at[len(moves) + 1]),
+    ]
+    for copy in leave:
+        copy.start()
+    loads[0].wait()
 
 
     entries = rbf.shape[0]
@@ -255,12 +279,13 @@
     def _():
         slots[...] = jnp.zeros_like(slots)
         for e in range(entries):
-            w_high, w_low = split(rbf[e])
-            high[e] = w_high
-            low[e] = w_low
+            w_high, w_low = split(weights[e])
             terms[e] = three_products(trace_out[face[e]], w_high, w_low, 0)
         for e in range(entries):
             slots[owner[e, 0] * blocks + node[e]] += terms[e]
+
+    for copy in leave:
+        copy.wait()
 
 
 def window(
@@ -278,14 +303,20 @@
             jax.ShapeDtypeStruct((rows, lanes), F32),
             jax.ShapeDtypeStruct((blocks, substeps, TILE), F32),
             jax.ShapeDtypeStruct((n_dom * blocks, substeps, TILE), F32),
-            jax.ShapeDtypeStruct(rbf.shape, BF16),
-            jax.ShapeDtypeStruct(rbf.shape, BF16),
         ),
-        in_specs=[pl.BlockSpec(memory_space=pltpu.SMEM)] * 3 + [vmem] * 9,
-        out_specs=(vmem,) * 6,
+        in_specs=[pl.BlockSpec(memory_space=pltpu.SMEM)] * 3
+        + [pl.BlockSpec(memory_space=pl.ANY)] * 9,
+        out_specs=(pl.BlockSpec(memory_space=pl.ANY),) * 2 + (vmem,) * 2,
         scratch_shapes=[pltpu.VMEM((rows + 2 * HALO, lanes + TILE), F32)] * 3
-        + [pltpu.VMEM((rbf.shape[0], substeps, TILE), F32)],
-        compiler_params=pltpu.CompilerParams(vmem_limit_bytes=40 * 1024 * 1024),
+        + [
+            pltpu.VMEM((rbf.shape[0], substeps, TILE), F32),
+            pltpu.VMEM(stiffness.shape, BF16),
+            pltpu.VMEM(wave.shape, F32),
+            pltpu.VMEM(wave.shape, F32),
+            pltpu.VMEM(rbf.shape, F32),
+            pltpu.SemaphoreType.DMA((18,)),
+        ],
+        compiler_params=pltpu.CompilerParams(vmem_limit_bytes=16 * 1024 * 1024),
         name="window",
     )(
         face, owner, node, state, previous, coefficient, stiffness, sides, wave, above, below,
@@ -417,8 +448,8 @@
     )(outgoing, trace)
 
 
-def pull_kernel(n_sect, n_dom, face, owner, node, loads, nodes, high, low, out, terms, sums):
-    entries = high.shape[0]
+def pull_kernel(n_sect, n_dom, face, owner, node, loads, nodes, rbf, out, terms, sums):
+    entries = rbf.shape[0]
     substeps = out.shape[0]
     blocks = loads.shape[0]
     d = lax.axis_index("dom")
@@ -435,7 +466,8 @@
         sums[...] = jnp.zeros_like(sums)
         for e in range(entries):
             slot = lax.rem(d - owner[e, 0] + n_dom, n_dom)
-            terms[e] = three_products(nodes[slot, node[e]], high[e], low[e], 1)
+            w_high, w_low = split(rbf[e])
+            terms[e] = three_products(nodes[slot, node[e]], w_high, w_low, 1)
         for e in range(entries):
             sums[face[e]] += terms[e]
         for b in range(blocks):
@@ -443,20 +475,20 @@
                 out[k, :, b * TILE : (b + 1) * TILE] = sums[b, k : k + 1, :]
 
 
-def pull(face, owner, node, loads, nodes, high, low, n_sect, n_dom):
+def pull(face, owner, node, loads, nodes, rbf, n_sect, n_dom):
     blocks, substeps, size = loads.shape
     return pl.pallas_call(
         functools.partial(pull_kernel, n_sect, n_dom),
         out_shape=jax.ShapeDtypeStruct((substeps, 1, blocks * size), F32),
         in_specs=[pl.BlockSpec(memory_space=pltpu.SMEM)] * 3
-        + [pl.BlockSpec(memory_space=pltpu.VMEM)] * 4,
+        + [pl.BlockSpec(memory_space=pltpu.VMEM)] * 3,
         out_specs=pl.BlockSpec(memory_space=pltpu.VMEM),
         scratch_shapes=[
-            pltpu.VMEM((high.shape[0], substeps, size), F32),
+            pltpu.VMEM((rbf.shape[0], substeps, size), F32),
             pltpu.VMEM((blocks, substeps, size), F32),
         ],
         name="pull",
-    )(face, owner, node, loads, nodes, high, low)
+    )(face, owner, node, loads, nodes, rbf)
 
 
 def local(
@@ -465,12 +497,12 @@
     n_sect = lax.axis_size("sect")
     n_dom = lax.axis_size("dom")
     sides, wave, above, below = exchange(state, previous, coefficient, waveform, n_sect, n_dom)
-    current, before, trace, outgoing, high, low = window(
+    current, before, trace, outgoing = window(
         entry_face, entry_owner, entry_node, state, previous, coefficient, stiffness, sides,
         wave, above, below, rbf, n_sect, n_dom,
     )
     loads, nodes = swap(outgoing, trace, n_sect, n_dom)
-    out = pull(entry_face, entry_owner, entry_node, loads, nodes, high, low, n_sect, n_dom)
+    out = pull(entry_face, entry_owner, entry_node, loads, nodes, rbf, n_sect, n_dom)
     return (current, before, out)
 
 

time: 49.9 us -> 49.4 us (0.990)
  local copies, waits for them, and re-layouts: 10.2 us -> 9.09 us
  Pallas kernels: 38.5 us -> 39.1 us
    unnamed x33 -> x29, local copies, waits for them, and re-layouts: 10.2 us -> 9.09 us
    pallas_call x1, Pallas kernels: 12.3 us -> 12.9 us  [swap(): pl.pallas_call(functools.partial(swap_kernel, n_sect, n_dom), out_shape=(...]
where the time goes in v3:
time: 49.4 us; the launch traced here: 48.9 us
  Pallas kernels  39.1 us (79%)
  local copies, waits for them, and re-layouts  9.09 us (18%)
  between operations  0.75 us (2%)
    pallas_call x1, Pallas kernels, swap(): pl.pallas_call(functools.partial(swap_kernel, n_sect, n_dom), out_shape=(...  12.9 us
    pallas_call x1, Pallas kernels, window(): pl.pallas_call(functools.partial(window_kernel, n_sect), out_shape=(jax.S...  11.6 us
    pallas_call x1, Pallas kernels, exchange(): pl.pallas_call(functools.partial(halo_kernel, n_sect, n_dom), out_shape=(...  10.5 us
    unnamed x29, local copies, waits for them, and re-layouts  9.09 us
    pallas_call x1, Pallas kernels, pull(): pl.pallas_call(functools.partial(pull_kernel, n_sect, n_dom), out_shape=j...  4.1 us

profile of v3, /device:TPU:0, one launch (start us, length us, event | category | flops | bytes accessed | tf_op | source)
XLA Modules:
  0.0 48.9 jit_solution(9566877330286896462)
XLA Ops:
  0.6 0.0 copy-start
  0.6 0.0 copy-start.13
  0.7 0.0 copy-start.12
  0.7 0.0 copy-start.1
  0.7 0.9 %copy.12.owner = s32[32,1]{1,0:T(8,128)S(1)} copy(s32[32,1]{0,1:T(1,128)} %param.15) | data formatting | bytes 256 | tf_op args[6]
  1.6 10.5 %halo.1 = (f32[3,512,128]{2,1,0:T(8,128)}, f32[8,640]{1,0:T(8,128)}, f32[32,640]{1,0:T(8,128)}, f32[24,640]{1,0:T(8,128)}) custom-call(f32[512,512]{1,0:T(8,128)} %state.1, f32[512,512]{1,0:T(8,128)} %previous.1, f32[512,512]{1,0:T(8,128)} %coefficient.1, f32[8,1,512]{2,1,0:T(1,128)} %refs_3_.1), custom_call_target="tpu_custom_call" | custom-call | tf_op jit(solution)/shard_map/halo/pallas_call | solution.py:152
  12.1 0.0 copy-done
  12.1 0.0 copy-done.13
  12.1 0.0 copy-done.12
  12.1 0.0 copy-done.1
  12.1 0.0 copy-start.2
  12.1 1.2 %copy-done.2 = f32[512,512]{1,0:T(8,128)S(1)} copy-done((f32[512,512]{1,0:T(8,128)S(1)}, f32[512,512]{1,0:T(8,128)}, u32[]{:S(2)}) %copy-start.2) | copy-done | bytes 1048600
  13.3 1.2 %copy-done.3 = f32[512,512]{1,0:T(8,128)S(1)} copy-done((f32[512,512]{1,0:T(8,128)S(1)}, f32[512,512]{1,0:T(8,128)}, u32[]{:S(2)}) %copy-start.3) | copy-done | bytes 1048600
  14.6 1.1 %copy-done.4 = f32[3,512,128]{2,1,0:T(8,128)S(1)} copy-done((f32[3,512,128]{2,1,0:T(8,128)S(1)}, f32[3,512,128]{2,1,0:T(8,128)}, u32[]{:S(2)}) %copy-start.4) | copy-done | bytes 786456
  15.7 0.9 %copy-done.7 = bf16[4,128,128]{2,1,0:T(8,128)(2,1)S(1)} copy-done((bf16[4,128,128]{2,1,0:T(8,128)(2,1)S(1)}, bf16[4,128,128]{2,1,0:T(8,128)(2,1)}, u32[]{:S(2)}) %copy-start.7) | copy-done | bytes 131096
  16.6 0.9 %copy-done.8 = f32[32,640]{1,0:T(8,128)S(1)} copy-done((f32[32,640]{1,0:T(8,128)S(1)}, f32[32,640]{1,0:T(8,128)}, u32[]{:S(2)}) %copy-start.8) | copy-done | bytes 81944
  17.5 0.8 %copy-done.9 = f32[24,640]{1,0:T(8,128)S(1)} copy-done((f32[24,640]{1,0:T(8,128)S(1)}, f32[24,640]{1,0:T(8,128)}, u32[]{:S(2)}) %copy-start.9) | copy-done | bytes 61464
  18.3 0.7 %copy-done.10 = f32[8,640]{1,0:T(8,128)S(1)} copy-done((f32[8,640]{1,0:T(8,128)S(1)}, f32[8,640]{1,0:T(8,128)}, u32[]{:S(2)}) %copy-start.10) | copy-done | bytes 20504
  19.0 11.6 %window.1 = (f32[512,512]{1,0:T(8,128)}, f32[512,512]{1,0:T(8,128)}, f32[4,8,128]{2,1,0:T(8,128)S(1)}, f32[32,8,128]{2,1,0:T(8,128)S(1)}) custom-call(s32[32]{0:T(128)S(1)} %copy-done.12, s32[32,1]{1,0:T(8,128)S(1)} %copy.12.owner, s32[32]{0:T(128)S(1)} %copy-done.13, f32[512,512]{1,0:T(8,128)S(1)} %copy-done.1, f32[512,512]{1,0:T(8,128)S(1)} %copy-done.2, ...), custom_call_target="tpu_custom_call" | custom-call | tf_op jit(solution)/shard_map/window/pallas_call | solution.py:299
  30.6 0.0 copy-done.5
  30.6 0.6 %copy-done.6 = f32[32,8,128]{2,1,0:T(8,128)} copy-done((f32[32,8,128]{2,1,0:T(8,128)}, f32[32,8,128]{2,1,0:T(8,128)S(1)}, u32[]{:S(2)}) %copy-start.6) | copy-done | bytes 131096
  31.3 0.6 %copy-done.11 = f32[4,8,128]{2,1,0:T(8,128)} copy-done((f32[4,8,128]{2,1,0:T(8,128)}, f32[4,8,128]{2,1,0:T(8,128)S(1)}, u32[]{:S(2)}) %copy-start.11) | copy-done | bytes 16408
  31.9 12.9 %swap.1 = (f32[4,8,128]{2,1,0:T(8,128)}, f32[8,4,8,128]{3,2,1,0:T(8,128)}) custom-call(f32[32,8,128]{2,1,0:T(8,128)} %copy-done.6, f32[4,8,128]{2,1,0:T(8,128)} %copy-done.11), custom_call_target="tpu_custom_call" | custom-call | tf_op jit(solution)/shard_map/swap/pallas_call | solution.py:423
  44.8 4.1 %pull.1 = f32[8,1,512]{2,1,0:T(1,128)} custom-call(s32[32]{0:T(128)} %face.3, s32[32,1]{1,0:T(8,128)} %copy-done.5, s32[32]{0:T(128)} %node.3, f32[4,8,128]{2,1,0:T(8,128)} %get-tuple-element.21.loads, f32[8,4,8,128]{3,2,1,0:T(8,128)} %get-tuple-element.22.nodes, f32[32,128,128]{2,1,0:T(8,128)} %rbf.3), custom_call_target="tpu_custom_call" | custom-call | tf_op jit(solution)/shard_map/pull/pallas_call | solution.py:480
  (9 shorter events, 0.0 us)
Async XLA Ops:
  0.6 11.4 %copy-start = (f32[32,128,128]{2,1,0:T(8,128)S(1)}, f32[32,128,128]{2,1,0:T(8,128)}, u32[]{:S(2)}) copy-start(f32[32,128,128]{2,1,0:T(8,128)} %rbf.3) | copy-start | bytes 6291460
  0.6 11.4 %copy-start.13 = (s32[32]{0:T(128)S(1)}, s32[32]{0:T(128)}, u32[]{:S(2)}) copy-start(s32[32]{0:T(128)} %node.3) | copy-start | bytes 388
  0.7 11.4 %copy-start.12 = (s32[32]{0:T(128)S(1)}, s32[32]{0:T(128)}, u32[]{:S(2)}) copy-start(s32[32]{0:T(128)} %face.3) | copy-start | bytes 388
  0.7 11.4 %copy-start.1 = (f32[512,512]{1,0:T(8,128)S(1)}, f32[512,512]{1,0:T(8,128)}, u32[]{:S(2)}) copy-start(f32[512,512]{1,0:T(8,128)} %state.1) | copy-start | bytes 3145732
  1.6 29.0 %copy-start.5 = (s32[32,1]{1,0:T(8,128)}, s32[32,1]{1,0:T(8,128)S(1)}, u32[]{:S(2)}) copy-start(s32[32,1]{1,0:T(8,128)S(1)} %copy.12.owner) | copy-start | bytes 388
  12.1 1.2 %copy-start.2 = (f32[512,512]{1,0:T(8,128)S(1)}, f32[512,512]{1,0:T(8,128)}, u32[]{:S(2)}) copy-start(f32[512,512]{1,0:T(8,128)} %previous.1) | copy-start | bytes 3145732
  13.3 1.2 %copy-start.3 = (f32[512,512]{1,0:T(8,128)S(1)}, f32[512,512]{1,0:T(8,128)}, u32[]{:S(2)}) copy-start(f32[512,512]{1,0:T(8,128)} %coefficient.1) | copy-start | bytes 3145732
  14.6 1.1 %copy-start.4 = (f32[3,512,128]{2,1,0:T(8,128)S(1)}, f32[3,512,128]{2,1,0:T(8,128)}, u32[]{:S(2)}) copy-start(f32[3,512,128]{2,1,0:T(8,128)} %get-tuple-element.13.sides) | copy-start | bytes 2359300
  15.7 0.9 %copy-start.7 = (bf16[4,128,128]{2,1,0:T(8,128)(2,1)S(1)}, bf16[4,128,128]{2,1,0:T(8,128)(2,1)}, u32[]{:S(2)}) copy-start(bf16[4,128,128]{2,1,0:T(8,128)(2,1)} %stiffness.1) | copy-start | bytes 393220
  16.6 0.9 %copy-start.8 = (f32[32,640]{1,0:T(8,128)S(1)}, f32[32,640]{1,0:T(8,128)}, u32[]{:S(2)}) copy-start(f32[32,640]{1,0:T(8,128)} %get-tuple-element.15.above) | copy-start | bytes 245764
  17.5 0.8 %copy-start.9 = (f32[24,640]{1,0:T(8,128)S(1)}, f32[24,640]{1,0:T(8,128)}, u32[]{:S(2)}) copy-start(f32[24,640]{1,0:T(8,128)} %get-tuple-element.16.below) | copy-start | bytes 184324
  18.3 0.7 %copy-start.10 = (f32[8,640]{1,0:T(8,128)S(1)}, f32[8,640]{1,0:T(8,128)}, u32[]{:S(2)}) copy-start(f32[8,640]{1,0:T(8,128)} %get-tuple-element.14.wave) | copy-start | bytes 61444
  30.6 0.7 %copy-start.6 = (f32[32,8,128]{2,1,0:T(8,128)}, f32[32,8,128]{2,1,0:T(8,128)S(1)}, u32[]{:S(2)}) copy-start(f32[32,8,128]{2,1,0:T(8,128)S(1)} %get-tuple-element.19.outgoing) | copy-start | bytes 393220
  31.3 0.6 %copy-start.11 = (f32[4,8,128]{2,1,0:T(8,128)}, f32[4,8,128]{2,1,0:T(8,128)S(1)}, u32[]{:S(2)}) copy-start(f32[4,8,128]{2,1,0:T(8,128)S(1)} %get-tuple-element.20.trace) | copy-start | bytes 49156

commit v4 on v3

--- a/solution.py
+++ b/solution.py
@@ -182,8 +182,8 @@
 
 def window_kernel(
     n_sect, face, owner, node, state, previous, coefficient, stiffness, sides, wave, above,
-    below, rbf, state_out, previous_out, trace_out, slots, first, second, coef, terms,
-    matrices, wave_own, wave_up, weights, sems,
+    below, rbf, state_out, previous_out, trace_hbm, slots_hbm, first, second, coef, terms,
+    matrices, wave_own, wave_up, weights, trace_out, slots, sems,
 ):
     rows, lanes = state.shape
     wide = lanes + TILE
@@ -266,6 +266,7 @@
     leave = [
         pltpu.make_async_copy(first.at[inner, left], state_out, sems.at[len(moves)]),
         pltpu.make_async_copy(second.at[inner, left], previous_out, sems.at[len(moves) + 1]),
+        pltpu.make_async_copy(trace_out, trace_hbm, sems.at[len(moves) + 2]),
     ]
     for copy in leave:
         copy.start()
@@ -275,15 +276,18 @@
     entries = rbf.shape[0]
     blocks = trace_out.shape[0]
 
+    slots[...] = jnp.zeros_like(slots)
+
     @pl.when(jnp.logical_not(on_shell))
     def _():
-        slots[...] = jnp.zeros_like(slots)
         for e in range(entries):
             w_high, w_low = split(weights[e])
             terms[e] = three_products(trace_out[face[e]], w_high, w_low, 0)
         for e in range(entries):
             slots[owner[e, 0] * blocks + node[e]] += terms[e]
 
+    leave.append(pltpu.make_async_copy(slots, slots_hbm, sems.at[len(moves) + 3]))
+    leave[-1].start()
     for copy in leave:
         copy.wait()
 
@@ -295,7 +299,6 @@
     rows, lanes = state.shape
     substeps = wave.shape[0]
     blocks = lanes // TILE
-    vmem = pl.BlockSpec(memory_space=pltpu.VMEM)
     return pl.pallas_call(
         functools.partial(window_kernel, n_sect),
         out_shape=(
@@ -305,8 +308,8 @@
             jax.ShapeDtypeStruct((n_dom * blocks, substeps, TILE), F32),
         ),
         in_specs=[pl.BlockSpec(memory_space=pltpu.SMEM)] * 3
-        + [pl.BlockSpec(memory_space=pl.ANY)] * 9,
-        out_specs=(pl.BlockSpec(memory_space=pl.ANY),) * 2 + (vmem,) * 2,
+        + [pl.BlockSpec(memory_space=pltpu.HBM)] * 9,
+        out_specs=(pl.BlockSpec(memory_space=pltpu.HBM),) * 4,
         scratch_shapes=[pltpu.VMEM((rows + 2 * HALO, lanes + TILE), F32)] * 3
         + [
             pltpu.VMEM((rbf.shape[0], substeps, TILE), F32),
@@ -314,9 +317,11 @@
             pltpu.VMEM(wave.shape, F32),
             pltpu.VMEM(wave.shape, F32),
             pltpu.VMEM(rbf.shape, F32),
-            pltpu.SemaphoreType.DMA((18,)),
+            pltpu.VMEM((blocks, substeps, TILE), F32),
+            pltpu.VMEM((n_dom * blocks, substeps, TILE), F32),
+            pltpu.SemaphoreType.DMA((20,)),
         ],
-        compiler_params=pltpu.CompilerParams(vmem_limit_bytes=16 * 1024 * 1024),
+        compiler_params=pltpu.CompilerParams(vmem_limit_bytes=60 * 1024 * 1024),
         name="window",
     )(
         face, owner, node, state, previous, coefficient, stiffness, sides, wave, above, below,

time: 49.4 us -> 42.6 us (0.86)
  local copies, waits for them, and re-layouts: 9.09 us -> 1.34 us
  Pallas kernels: 39.1 us -> 40.3 us
    unnamed x29 -> x1, local copies, waits for them, and re-layouts: 9.09 us -> 1.34 us
    pallas_call x1, Pallas kernels: 11.6 us -> 13.1 us  [window(): pl.pallas_call(functools.partial(window_kernel, n_sect), out_shape=(jax.S...]
where the time goes in v4:
time: 42.6 us; the launch traced here: 42.3 us
  Pallas kernels  40.3 us (95%)
  local copies, waits for them, and re-layouts  1.34 us (3%)
  between operations  0.65 us (2%)
    pallas_call x1, Pallas kernels, window(): pl.pallas_call(functools.partial(window_kernel, n_sect), out_shape=(jax.S...  13.1 us
    pallas_call x1, Pallas kernels, swap(): pl.pallas_call(functools.partial(swap_kernel, n_sect, n_dom), out_shape=(...  12.7 us
    pallas_call x1, Pallas kernels, exchange(): pl.pallas_call(functools.partial(halo_kernel, n_sect, n_dom), out_shape=(...  10.4 us
    pallas_call x1, Pallas kernels, pull(): pl.pallas_call(functools.partial(pull_kernel, n_sect, n_dom), out_shape=j...  4.1 us
    unnamed x1, local copies, waits for them, and re-layouts  1.34 us

profile of v4, /device:TPU:0, one launch (start us, length us, event | category | flops | bytes accessed | tf_op | source)
XLA Modules:
  0.0 42.3 jit_solution(4360971355045278662)
XLA Ops:
  0.6 1.3 %copy.12.owner = s32[32,1]{1,0:T(8,128)} copy(s32[32,1]{0,1:T(1,128)} %param.15) | data formatting | bytes 256 | tf_op args[6]
  2.0 10.4 %halo.1 = (f32[3,512,128]{2,1,0:T(8,128)}, f32[8,640]{1,0:T(8,128)}, f32[32,640]{1,0:T(8,128)}, f32[24,640]{1,0:T(8,128)}) custom-call(f32[512,512]{1,0:T(8,128)} %state.1, f32[512,512]{1,0:T(8,128)} %previous.1, f32[512,512]{1,0:T(8,128)} %coefficient.1, f32[8,1,512]{2,1,0:T(1,128)} %refs_3_.1), custom_call_target="tpu_custom_call" | custom-call | tf_op jit(solution)/shard_map/halo/pallas_call | solution.py:152
  12.4 13.1 %window.1 = (f32[512,512]{1,0:T(8,128)}, f32[512,512]{1,0:T(8,128)}, f32[4,8,128]{2,1,0:T(8,128)}, f32[32,8,128]{2,1,0:T(8,128)}) custom-call(s32[32]{0:T(128)} %face.3, s32[32,1]{1,0:T(8,128)} %copy.12.owner, s32[32]{0:T(128)} %node.3, f32[512,512]{1,0:T(8,128)} %state.1, f32[512,512]{1,0:T(8,128)} %previous.1, f32[512,512]{1,0:T(8,128)} %coefficient.1, ...), custom_call_target="tpu_custom_call" | custom-call | tf_op jit(solution)/shard_map/window/pallas_call | solution.py:302
  25.5 12.7 %swap.1 = (f32[4,8,128]{2,1,0:T(8,128)}, f32[8,4,8,128]{3,2,1,0:T(8,128)}) custom-call(f32[32,8,128]{2,1,0:T(8,128)} %get-tuple-element.19.outgoing, f32[4,8,128]{2,1,0:T(8,128)} %get-tuple-element.20.trace), custom_call_target="tpu_custom_call" | custom-call | tf_op jit(solution)/shard_map/swap/pallas_call | solution.py:428
  38.2 4.1 %pull.1 = f32[8,1,512]{2,1,0:T(1,128)} custom-call(s32[32]{0:T(128)} %face.3, s32[32,1]{1,0:T(8,128)} %copy.12.owner, s32[32]{0:T(128)} %node.3, f32[4,8,128]{2,1,0:T(8,128)} %get-tuple-element.21.loads, f32[8,4,8,128]{3,2,1,0:T(8,128)} %get-tuple-element.22.nodes, f32[32,128,128]{2,1,0:T(8,128)} %rbf.3), custom_call_target="tpu_custom_call" | custom-call | tf_op jit(solution)/shard_map/pull/pallas_call | solution.py:485

commit v5 on v4

--- a/solution.py
+++ b/solution.py
@@ -36,7 +36,7 @@
     sides_ref, wave_out, above_ref, below_ref = refs[4:8]
     to_left, to_right, from_left, from_right, to_up, to_down, from_up, from_down = refs[8:16]
     from_up_left, from_up_right, from_down_left, from_down_right = refs[16:20]
-    send_sem, recv_sem = refs[20:22]
+    send_sem, recv_sem, tiles, edge_sem = refs[20:24]
     s = lax.axis_index("sect")
     d = lax.axis_index("dom")
     rows, lanes = fields[0].shape
@@ -70,26 +70,36 @@
             signal(barrier, section, column)
 
     wave = jnp.concatenate([wave_ref[k] for k in range(substeps)], 0)
+    edges = []
     for a in range(3):
         part = pl.ds(a * HALO, HALO)
-        to_up[part] = fields[a][:HALO]
-        to_down[part] = fields[a][rows - HALO :]
+        for source, target in (
+            (fields[a].at[:, first], tiles.at[0, a]),
+            (fields[a].at[:, last], tiles.at[1, a]),
+            (fields[a].at[pl.ds(0, HALO)], to_up.at[part]),
+            (fields[a].at[pl.ds(rows - HALO, HALO)], to_down.at[part]),
+        ):
+            copy = pltpu.make_async_copy(source, target, edge_sem.at[len(edges)])
+            copy.start()
+            edges.append(copy)
     to_down[3 * HALO :] = wave
+    for copy in edges:
+        copy.wait()
     lane = lax.broadcasted_iota(jnp.int32, (rows, TILE), 1)
 
     def pack(where, start):
-        a = fields[0][:, where]
-        b = pltpu.roll(fields[1][:, where], (HALO - start) % TILE, 1)
-        c = pltpu.roll(fields[2][:, where], (2 * HALO - start) % TILE, 1)
+        a = tiles[where, 0]
+        b = pltpu.roll(tiles[where, 1], (HALO - start) % TILE, 1)
+        c = pltpu.roll(tiles[where, 2], (2 * HALO - start) % TILE, 1)
         if start:
             a = pltpu.roll(a, TILE - start, 1)
         packed = jnp.where(lane < HALO, a, jnp.where(lane < 2 * HALO, b, c))
         return packed.T[: 3 * HALO]
 
-    to_left[: 3 * HALO] = pack(first, 0)
+    to_left[: 3 * HALO] = pack(0, 0)
     to_left[3 * HALO :, :TILE] = wave[:, :TILE]
     to_left[3 * HALO :, TILE:] = jnp.zeros((HALO, rows - TILE), F32)
-    to_right[: 3 * HALO] = pack(last, TILE - HALO)
+    to_right[: 3 * HALO] = pack(1, TILE - HALO)
     to_right[3 * HALO :, :TILE] = wave[:, lanes - TILE :]
     to_right[3 * HALO :, TILE:] = jnp.zeros((HALO, rows - TILE), F32)
 
@@ -157,7 +167,7 @@
             jax.ShapeDtypeStruct((4 * HALO, wide), F32),
             jax.ShapeDtypeStruct((3 * HALO, wide), F32),
         ),
-        in_specs=[vmem] * 4,
+        in_specs=[pl.BlockSpec(memory_space=pl.ANY)] * 3 + [vmem],
         out_specs=(vmem,) * 4,
         scratch_shapes=[pltpu.VMEM((4 * HALO, rows), F32)] * 4
         + [
@@ -171,8 +181,12 @@
             pltpu.VMEM((3 * HALO, TILE), F32),
             pltpu.SemaphoreType.DMA((8,)),
             pltpu.SemaphoreType.DMA((8,)),
+            pltpu.VMEM((2, 3, rows, TILE), F32),
+            pltpu.SemaphoreType.DMA((12,)),
         ],
-        compiler_params=pltpu.CompilerParams(collective_id=0, has_side_effects=True),
+        compiler_params=pltpu.CompilerParams(
+            collective_id=0, has_side_effects=True, vmem_limit_bytes=60 * 1024 * 1024
+        ),
         name="halo",
     )(state, previous, coefficient, wave)
 

time: 42.6 us -> 41.6 us (0.977)
  Pallas kernels: 40.3 us -> 39.3 us
    pallas_call x1, Pallas kernels: 10.4 us -> 9.71 us  [exchange(): pl.pallas_call(functools.partial(halo_kernel, n_sect, n_dom), out_shape=(...]
where the time goes in v5:
time: 41.6 us; the launch traced here: 41.2 us
  Pallas kernels  39.3 us (94%)
  local copies, waits for them, and re-layouts  1.34 us (3%)
  between operations  0.65 us (2%)
    pallas_call x1, Pallas kernels, window(): pl.pallas_call(functools.partial(window_kernel, n_sect), out_shape=(jax.S...  13.1 us
    pallas_call x1, Pallas kernels, swap(): pl.pallas_call(functools.partial(swap_kernel, n_sect, n_dom), out_shape=(...  12.3 us
    pallas_call x1, Pallas kernels, exchange(): pl.pallas_call(functools.partial(halo_kernel, n_sect, n_dom), out_shape=(...  9.71 us
    pallas_call x1, Pallas kernels, pull(): pl.pallas_call(functools.partial(pull_kernel, n_sect, n_dom), out_shape=j...  4.09 us
    unnamed x1, local copies, waits for them, and re-layouts  1.34 us

profile of v5, /device:TPU:0, one launch (start us, length us, event | category | flops | bytes accessed | tf_op | source)
XLA Modules:
  0.0 41.2 jit_solution(7120776368936687460)
XLA Ops:
  0.6 1.3 %copy.12.owner = s32[32,1]{1,0:T(8,128)} copy(s32[32,1]{0,1:T(1,128)} %param.15) | data formatting | bytes 256 | tf_op args[6]
  2.0 9.7 %halo.1 = (f32[3,512,128]{2,1,0:T(8,128)}, f32[8,640]{1,0:T(8,128)}, f32[32,640]{1,0:T(8,128)}, f32[24,640]{1,0:T(8,128)}) custom-call(f32[512,512]{1,0:T(8,128)} %state.1, f32[512,512]{1,0:T(8,128)} %previous.1, f32[512,512]{1,0:T(8,128)} %coefficient.1, f32[8,1,512]{2,1,0:T(1,128)} %refs_3_.1), custom_call_target="tpu_custom_call" | custom-call | tf_op jit(solution)/shard_map/halo/pallas_call | solution.py:162
  11.7 13.1 %window.1 = (f32[512,512]{1,0:T(8,128)}, f32[512,512]{1,0:T(8,128)}, f32[4,8,128]{2,1,0:T(8,128)}, f32[32,8,128]{2,1,0:T(8,128)}) custom-call(s32[32]{0:T(128)} %face.3, s32[32,1]{1,0:T(8,128)} %copy.12.owner, s32[32]{0:T(128)} %node.3, f32[512,512]{1,0:T(8,128)} %state.1, f32[512,512]{1,0:T(8,128)} %previous.1, f32[512,512]{1,0:T(8,128)} %coefficient.1, ...), custom_call_target="tpu_custom_call" | custom-call | tf_op jit(solution)/shard_map/window/pallas_call | solution.py:316
  24.8 12.3 %swap.1 = (f32[4,8,128]{2,1,0:T(8,128)}, f32[8,4,8,128]{3,2,1,0:T(8,128)}) custom-call(f32[32,8,128]{2,1,0:T(8,128)} %get-tuple-element.19.outgoing, f32[4,8,128]{2,1,0:T(8,128)} %get-tuple-element.20.trace), custom_call_target="tpu_custom_call" | custom-call | tf_op jit(solution)/shard_map/swap/pallas_call | solution.py:442
  37.2 4.1 %pull.1 = f32[8,1,512]{2,1,0:T(1,128)} custom-call(s32[32]{0:T(128)} %face.3, s32[32,1]{1,0:T(8,128)} %copy.12.owner, s32[32]{0:T(128)} %node.3, f32[4,8,128]{2,1,0:T(8,128)} %get-tuple-element.21.loads, f32[8,4,8,128]{3,2,1,0:T(8,128)} %get-tuple-element.22.nodes, f32[32,128,128]{2,1,0:T(8,128)} %rbf.3), custom_call_target="tpu_custom_call" | custom-call | tf_op jit(solution)/shard_map/pull/pallas_call | solution.py:499
